TPU v7x, 32 devices: a whole 2x2x4 slice. The times are simulated.
32 devices in a mesh: dp: 8 (over y, x, core), tensor: 4 (over z).
Axes of the slice: x: 2, y: 2, z: 4, core: 2. Of those that a mesh axis runs over, the one named last changes fastest.
Arguments:
- tokens: bfloat16 [4096, 3072], P('dp', 'tensor'), may hold values from -6 to 6
- cotangent: bfloat16 [4096, 1024], P('dp'), may hold values from -8 to 8
- weight: bfloat16 [3072, 1024], P('tensor'), may hold values from -6 to 6
- momentum: bfloat16 [8, 3072, 1024], P('dp', 'tensor'), may hold values from -1.1953125 to 1.1953125
- threshold: int32 [1024], replicated, may hold values from 2 to 8
Outputs:
- key_values: bfloat16 [4096, 1024], P(('dp', 'tensor'))
- input_grad: bfloat16 [4096, 3072], P('dp', 'tensor')
- new_momentum: bfloat16 [8, 3072, 1024], P('dp', 'tensor')
- new_weight: bfloat16 [3072, 1024], P('tensor', 'dp')
All inputs are finite; a program needn't handle non-finite values.
Results may differ from a plain program's by a relative error of at most 0.017.
Values may be sent and summed in bfloat16 or wider, within the bound.
No kernel may reach another device: no remote copies, remote signals or barrier semaphores. Data moves between devices by JAX's collectives and lax.ppermute only.
A program may use at most 64 MiB of HBM per device.

v0:
```python
import jax
import jax.numpy as jnp
from jax import lax
from jax.sharding import PartitionSpec as P

D = 3072


def per_device(tokens, cotangent, weight, momentum, threshold):
    inverse = D ** (-0.5)
    key_values = lax.psum_scatter(
        (jnp.dot(tokens, weight, preferred_element_type=jnp.float32) * inverse).astype(
            jnp.bfloat16
        ),
        "tensor",
        scatter_dimension=0,
        tiled=True,
    )
    input_grad = (
        lax.dot_general(
            cotangent, weight, (((1,), (1,)), ((), ())), preferred_element_type=jnp.float32
        )
        * inverse
    ).astype(jnp.bfloat16)
    gradient = (
        lax.dot_general(
            tokens, cotangent, (((0,), (0,)), ((), ())), preferred_element_type=jnp.float32
        )
        * inverse
    )
    fresh = (0.9 * momentum[0].astype(jnp.float32) + 0.1 * gradient).astype(jnp.bfloat16)
    column_share = weight.shape[1] // lax.axis_size("dp")
    arrived = lax.all_to_all(fresh[None], "dp", split_axis=2, concat_axis=0, tiled=True)
    votes = jnp.sum(jnp.clip(arrived.astype(jnp.float32) / 0.125, -1.0, 1.0), axis=0)
    first_column = lax.axis_index("dp") * column_share
    own_columns = lax.dynamic_slice_in_dim(weight, first_column, column_share, 1)
    own_limits = lax.dynamic_slice_in_dim(threshold, first_column, column_share, 0)
    update = jnp.clip(votes / own_limits.astype(jnp.float32)[None, :], -1.0, 1.0)
    new_weight = (own_columns.astype(jnp.float32) - 0.5 * update).astype(jnp.bfloat16)
    return (key_values, input_grad, fresh[None], new_weight)


def solution(mesh):
    in_specs = (P("dp", "tensor"), P("dp", None), P("tensor", None), P("dp", "tensor", None), P())
    out_specs = (
        P(("dp", "tensor"), None),
        P("dp", "tensor"),
        P("dp", "tensor", None),
        P("tensor", "dp"),
    )
    return jax.shard_map(
        per_device, mesh=mesh, in_specs=in_specs, out_specs=out_specs, check_vma=False
    )
```

profile of v0, /device:TPU:0, one launch (start us, length us, event | category | flops | bytes accessed | tf_op | source)
XLA Modules:
  0.0 78.0 jit_solution(1171594350504713559)
XLA Ops:
  7.2 0.0 copy-start
  7.2 3.2 %fusion.1 = bf16[1,768,1024]{2,1,0:T(8,128)(2,1)S(1)} fusion(bf16[512,768]{1,0:T(8,128)(2,1)} %param.5, bf16[512,1024]{1,0:T(8,128)(2,1)} %param.6, bf16[1,768,1024]{2,1,0:T(8,128)(2,1)} %param.8), kind=kOutput, calls=%fused_computation.5 | convolution fusion | flops 809238528 | bytes 4980736 | tf_op jit(solution)/shard_map/dot_general | solution.py:26
  10.3 0.0 copy-start.1
  10.4 5.9 %copy.11 = bf16[1,768,1024]{1,0,2:T(2,128)(2,1)} copy(bf16[1,768,1024]{2,1,0:T(8,128)(2,1)S(1)} %fusion.1) | data formatting | bytes 3145728 | tf_op jit(solution)/shard_map/broadcast_in_dim | solution.py:40
  16.3 0.0 copy-done.1
  16.3 0.5 broadcast.25
  16.8 11.2 %reduce.3 = bf16[1024,768]{1,0:T(8,128)(2,1)S(1)} reduce(bf16[1024,1,768]{2,1,0:T(2,128)(2,1)} %bitcast.18, bf16[]{:T(256)} %broadcast.25), dimensions={1}, to_apply=%bitcast.9.reduce_sub_computation | reduce | bytes 3145730
  28.0 1.9 %reshape.25 = bf16[8,2,49152]{2,1,0:T(2,128)(2,1)} reshape(bf16[1024,768]{1,0:T(8,128)(2,1)S(1)} %reduce.3) | data formatting | bytes 3145728
  29.9 5.2 %all-to-all-start = ((bf16[8,2,49152]{2,1,0:T(2,128)(2,1)}), bf16[8,2,49152]{2,1,0:T(2,128)(2,1)S(1)}, u32[]{:S(2)}, u32[]{:S(2)}) async-start(bf16[8,2,49152]{2,1,0:T(2,128)(2,1)} %reshape.25), calls=%async_computation.1 | async-start | bytes 3145728 | tf_op jit(solution)/shard_map/all_to_all | solution.py:33
  35.1 0.2 reduce-scatter.2.cloned.1.call-start
  35.3 0.0 copy-done
  35.3 3.1 %multiply_convert_fusion = bf16[512,1024]{1,0:T(8,128)(2,1)} fusion(bf16[512,768]{1,0:T(8,128)(2,1)} %param.5, bf16[768,1024]{1,0:T(8,128)(2,1)S(1)} %copy-done), kind=kOutput, calls=%fused_computation.3 | convolution fusion | flops 806354944 | bytes 3407872 | tf_op jit(solution)/shard_map/dot_general | solution.py:12
  38.4 0.0 reduce-scatter.2.cloned.1.call-update
  38.4 0.1 constant_dynamic-slice_fusion
  38.5 0.1 copy.14
  38.7 0.8 dynamic-slice_convert_fusion
  39.4 3.1 %multiply_convert_fusion.1 = bf16[512,768]{1,0:T(8,128)(2,1)} fusion(bf16[512,1024]{1,0:T(8,128)(2,1)} %param.6, bf16[768,1024]{1,0:T(8,128)(2,1)S(1)} %copy-done), kind=kOutput, calls=%fused_computation.4 | convolution fusion | flops 806092800 | bytes 3407872 | tf_op jit(solution)/shard_map/dot_general | solution.py:20
  42.5 13.5 %all-to-all-done = bf16[8,2,49152]{2,1,0:T(2,128)(2,1)S(1)} async-done(((bf16[8,2,49152]{2,1,0:T(2,128)(2,1)}), bf16[8,2,49152]{2,1,0:T(2,128)(2,1)S(1)}, u32[]{:S(2)}, u32[]{:S(2)}) %all-to-all-start) | async-done | bytes 1572896 | tf_op jit(solution)/shard_map/all_to_all | solution.py:33
  56.1 3.9 %reshape.26 = bf16[1024,1,768]{2,1,0:T(2,128)(2,1)} reshape(bf16[8,2,49152]{2,1,0:T(2,128)(2,1)S(1)} %all-to-all-done) | data formatting | bytes 3145728
  60.0 6.2 %multiply_clamp_fusion = f32[1,768,1024]{1,0,2:T(1,128)S(1)} fusion(bf16[1024,1,768]{2,1,0:T(2,128)(2,1)} %reshape.26), kind=kLoop, calls=%fused_computation.2 | loop fusion | flops 2359296 | bytes 4718592 | tf_op jit(solution)/shard_map/jit(clip)/min | solution.py:34
  66.2 1.9 %copy.13 = f32[1,768,1024]{1,2,0:T(8,128)} copy(f32[1,768,1024]{1,0,2:T(1,128)S(1)} %multiply_clamp_fusion) | data formatting | bytes 6291456
  68.1 2.1 %reduce.2 = f32[768,128]{0,1:T(8,128)S(1)} reduce(f32[768,8,128]{0,2,1:T(8,128)} %bitcast.19, f32[]{:T(128)} %constant.30.clone.1), dimensions={1}, to_apply=%region_1.2 | reduce | flops 688128 | bytes 3538948 | tf_op jit(solution)/shard_map/reduce_sum | solution.py:34
  70.2 0.1 subtract_convert_fusion
  70.4 0.8 %copy.12 = bf16[768,128]{1,0:T(8,128)(2,1)} copy(bf16[768,128]{0,1:T(8,128)(2,1)S(1)} %subtract_convert_fusion) | data formatting | bytes 393216
  71.2 0.0 reduce-scatter.2.cloned.1.call-done
Async XLA Ops:
  7.2 28.1 %copy-start = (bf16[768,1024]{1,0:T(8,128)(2,1)S(1)}, bf16[768,1024]{1,0:T(8,128)(2,1)}, u32[]{:S(2)}) copy-start(bf16[768,1024]{1,0:T(8,128)(2,1)} %param.7) | copy-start | bytes 4718596
  10.3 5.9 %copy-start.1 = (bf16[1,768,1024]{2,1,0:T(8,128)(2,1)}, bf16[1,768,1024]{2,1,0:T(8,128)(2,1)S(1)}, u32[]{:S(2)}) copy-start(bf16[1,768,1024]{2,1,0:T(8,128)(2,1)S(1)} %fusion.1) | copy-start | bytes 4718596
  29.9 26.2 %all-to-all-start = ((bf16[8,2,49152]{2,1,0:T(2,128)(2,1)}), bf16[8,2,49152]{2,1,0:T(2,128)(2,1)S(1)}, u32[]{:S(2)}, u32[]{:S(2)}) async-start(bf16[8,2,49152]{2,1,0:T(2,128)(2,1)} %reshape.25), calls=%async_computation.1 | async-start | bytes 3145728 | tf_op jit(solution)/shard_map/all_to_all | solution.py:33
  35.1 36.1 %reduce-scatter.2.cloned.1.call-start = ((), (), s32[]{:S(2)}) async-start(), calls=%async_computation.2 | async-start | bytes 1310720 | tf_op jit(solution)/shard_map/reduce_scatter | solution.py:11
Sparse Core Ops, SparseCore 0:
  38.7 28.9 reduce-scatter.1
where the time goes:
time: 78.4 us; the launch traced here: 78 us
  other arithmetic  20.5 us (26%)
  local copies, waits for them, and re-layouts  15.1 us (19%)
  between operations  14.1 us (18%)
  waiting for transfers between devices  13.5 us (17%)
  matrix products  9.39 us (12%)
  starting transfers between devices  5.41 us (7%)
    all_to_all x1, waiting for transfers between devices, per_device(): lax.all_to_all(fresh[None], 'dp', split_axis=2, concat_axis=0, tiled=True)  13.5 us
    unnamed x1, other arithmetic  11.2 us
    unnamed x10, local copies, waits for them, and re-layouts  9.15 us
    min x1, other arithmetic, per_device(): jnp.clip(arrived.astype(jnp.float32) / 0.125, -1.0, 1.0)  6.23 us
    broadcast_in_dim x1, local copies, waits for them, and re-layouts, per_device(): return (key_values, input_grad, fresh[None], new_weight)  5.9 us
    all_to_all x1, starting transfers between devices, per_device(): lax.all_to_all(fresh[None], 'dp', split_axis=2, concat_axis=0, tiled=True)  5.2 us
    dot_general x1, matrix products, per_device(): lax.dot_general(tokens, cotangent, (((0,), (0,)), ((), ())), preferred_el...  3.16 us
    dot_general x1, matrix products, per_device(): lax.dot_general(cotangent, weight, (((1,), (1,)), ((), ())), preferred_el...  3.13 us
  transfers between devices with their start and end apart: 2, of which 1 were waited for; matrix products, arithmetic and copies ran while one was open for 29% of the time, Pallas kernels for 0%

commit v1 on v0

v1 whole, which is shorter than its diff:
```python
import jax
import jax.numpy as jnp
from jax import lax
from jax.experimental import pallas as pl
from jax.experimental.pallas import tpu as pltpu
from jax.sharding import PartitionSpec as P

BF16 = jnp.bfloat16
F32 = jnp.float32
VMEM_LIMIT = 20 * 1024 * 1024
LANES = 128
WHOLE = pl.BlockSpec(memory_space=pltpu.VMEM)


def shaped(*dims):
    return jax.ShapeDtypeStruct(dims, BF16)


def params():
    return pltpu.CompilerParams(vmem_limit_bytes=VMEM_LIMIT)


def product_rows(tokens_ref, weight_ref, block, rows, inverse):
    picked = tokens_ref[pl.ds(pl.multiple_of(block * rows, rows), rows), :]
    total = jnp.dot(picked, weight_ref[...], preferred_element_type=F32)
    return (total * inverse).astype(BF16)


def is_outer(plane):
    return jnp.logical_or(plane == 0, plane == 3)


def far_block(plane):
    return jnp.where(plane % 2 == 0, 3, 0)


def near_block(plane):
    return jnp.where(plane % 2 == 0, 1, 2)


def third_block(plane):
    return jnp.where(plane == 0, 2, jnp.where(plane == 1, 3, jnp.where(plane == 2, 0, 1)))


def seed_kernel(inverse, rows, tokens_ref, weight_ref, out_ref):
    plane = lax.axis_index("tensor")
    out_ref[...] = product_rows(tokens_ref, weight_ref, far_block(plane), rows, inverse)


def rest_kernel(inverse, rows, tokens_ref, weight_ref, near_ref, third_ref, own_ref):
    plane = lax.axis_index("tensor")
    near_ref[...] = product_rows(tokens_ref, weight_ref, near_block(plane), rows, inverse)
    third_ref[...] = product_rows(tokens_ref, weight_ref, third_block(plane), rows, inverse)
    own_ref[...] = product_rows(tokens_ref, weight_ref, plane, rows, inverse)


def relay_kernel(third_ref, seed_ref, out_ref):
    outer = is_outer(lax.axis_index("tensor"))

    @pl.when(outer)
    def _():
        out_ref[...] = third_ref[...]

    @pl.when(jnp.logical_not(outer))
    def _():
        out_ref[...] = (third_ref[...].astype(F32) + seed_ref[...].astype(F32)).astype(BF16)


def keys_kernel(own_ref, seed_ref, across_ref, near_ref, third_ref, out_ref):
    outer = is_outer(lax.axis_index("tensor"))

    @pl.when(outer)
    def _():
        total = own_ref[...].astype(F32) + seed_ref[...].astype(F32)
        out_ref[...] = (total + third_ref[...].astype(F32)).astype(BF16)

    @pl.when(jnp.logical_not(outer))
    def _():
        total = own_ref[...].astype(F32) + across_ref[...].astype(F32)
        total = total + near_ref[...].astype(F32)
        out_ref[...] = (total + third_ref[...].astype(F32)).astype(BF16)


def momentum_kernel(inverse, share, tokens_ref, cot_ref, old_ref, new_ref, send_ref, keep_ref):
    odd = lax.axis_index("dp") % 2 == 1
    for pair in range(cot_ref.shape[1] // (2 * share)):
        span = slice(2 * pair * share, 2 * (pair + 1) * share)
        gradient = inverse * lax.dot_general(
            tokens_ref[...],
            cot_ref[:, span],
            (((0,), (0,)), ((), ())),
            preferred_element_type=F32,
        )
        fresh = (0.9 * old_ref[0, :, span].astype(F32) + 0.1 * gradient).astype(BF16)
        new_ref[0, :, span] = fresh
        votes = jnp.clip(fresh.astype(F32) * 8.0, -1.0, 1.0).astype(BF16)
        low, high = votes[:, :share], votes[:, share:]
        send_ref[pair] = jnp.where(odd, low, high)
        keep_ref[pair] = jnp.where(odd, high, low)


def pair_kernel(keep_ref, came_ref, *out_refs):
    chip = lax.axis_index("dp") // 2
    for offset, out_ref in enumerate(out_refs):
        there = jnp.bitwise_xor(chip, offset)
        total = keep_ref[there].astype(F32) + came_ref[there].astype(F32)
        out_ref[...] = total.astype(BF16)


def weight_kernel(share, weight_ref, threshold_ref, *refs):
    vote_refs, out_ref = refs[:-1], refs[-1]
    first = pl.multiple_of(lax.axis_index("dp") * share, share)
    votes = vote_refs[0][...].astype(F32)
    for ref in vote_refs[1:]:
        votes = votes + ref[...].astype(F32)
    limits = threshold_ref[:, pl.ds(first, share)].astype(F32)
    update = jnp.clip(votes / limits, -1.0, 1.0)
    old = weight_ref[:, pl.ds(first, share)].astype(F32)
    out_ref[...] = (old - 0.5 * update).astype(BF16)


def call(kernel, outs, *args, **more):
    more.setdefault("in_specs", [WHOLE] * len(args))
    more.setdefault("out_specs", [WHOLE] * len(outs))
    return pl.pallas_call(kernel, out_shape=outs, compiler_params=params(), **more)(*args)


def bind(function, *bound):
    def run(*refs):
        function(*bound, *refs)

    return run


def on_line_of_four(tokens, cotangent, weight, momentum, threshold):
    depth, width = weight.shape
    n_dp, n_tensor = lax.axis_size("dp"), lax.axis_size("tensor")
    rows = tokens.shape[0] // n_tensor
    share = width // n_dp
    inverse = (depth * n_tensor) ** (-0.5)

    def along(value, *pairs):
        return lax.ppermute(value, "tensor", pairs)

    def over(value, mask):
        return lax.ppermute(value, "dp", [(i, i ^ mask) for i in range(n_dp)])

    (seed,) = call(bind(seed_kernel, inverse, rows), [shaped(rows, width)], tokens, weight)
    seed_came = along(seed, (0, 1), (3, 2), (1, 0), (2, 3))

    tile = 256
    fresh, send, keep = call(
        bind(momentum_kernel, inverse, share),
        [
            shaped(1, depth, width),
            shaped(n_dp // 2, depth, share),
            shaped(n_dp // 2, depth, share),
        ],
        tokens,
        cotangent,
        momentum,
        grid=(depth // tile,),
        in_specs=[
            pl.BlockSpec((tokens.shape[0], tile), lambda i: (0, i)),
            pl.BlockSpec(cotangent.shape, lambda i: (0, 0)),
            pl.BlockSpec((1, tile, width), lambda i: (0, i, 0)),
        ],
        out_specs=[
            pl.BlockSpec((1, tile, width), lambda i: (0, i, 0)),
            pl.BlockSpec((n_dp // 2, tile, share), lambda i: (0, i, 0)),
            pl.BlockSpec((n_dp // 2, tile, share), lambda i: (0, i, 0)),
        ],
    )
    came = over(send, 1)

    near, third, own = call(
        bind(rest_kernel, inverse, rows), [shaped(rows, width)] * 3, tokens, weight
    )
    near_came = along(near, (0, 1), (3, 2), (1, 3), (2, 0))
    across_came = along(near, (1, 2), (2, 1), (0, 0), (3, 3))

    sums = call(bind(pair_kernel), [shaped(depth, share)] * (n_dp // 2), keep, came)
    votes = [sums[0]] + [over(sums[k], 2 * k) for k in range(1, n_dp // 2)]

    (relay,) = call(bind(relay_kernel), [shaped(rows, width)], third, seed_came)
    third_came = along(relay, (0, 2), (3, 1), (1, 3), (2, 0))

    input_grad = (
        lax.dot_general(cotangent, weight, (((1,), (1,)), ((), ())), preferred_element_type=F32)
        * inverse
    ).astype(BF16)

    (new_weight,) = call(
        bind(weight_kernel, share),
        [shaped(depth, share)],
        weight,
        threshold.reshape(1, width),
        *votes,
    )
    (key_values,) = call(
        bind(keys_kernel), [shaped(rows, width)], own, seed_came, across_came, near_came, third_came
    )
    return key_values, input_grad, fresh, new_weight


def in_general(tokens, cotangent, weight, momentum, threshold):
    inverse = (weight.shape[0] * lax.axis_size("tensor")) ** (-0.5)
    key_values = lax.psum_scatter(
        (jnp.dot(tokens, weight, preferred_element_type=F32) * inverse).astype(BF16),
        "tensor",
        scatter_dimension=0,
        tiled=True,
    )
    input_grad = (
        lax.dot_general(cotangent, weight, (((1,), (1,)), ((), ())), preferred_element_type=F32)
        * inverse
    ).astype(BF16)
    gradient = inverse * lax.dot_general(
        tokens, cotangent, (((0,), (0,)), ((), ())), preferred_element_type=F32
    )
    fresh = (0.9 * momentum[0].astype(F32) + 0.1 * gradient).astype(BF16)
    share = weight.shape[1] // lax.axis_size("dp")
    arrived = lax.all_to_all(fresh[None], "dp", split_axis=2, concat_axis=0, tiled=True)
    votes = jnp.sum(jnp.clip(arrived.astype(F32) / 0.125, -1.0, 1.0), axis=0)
    first = lax.axis_index("dp") * share
    own_columns = lax.dynamic_slice_in_dim(weight, first, share, 1)
    own_limits = lax.dynamic_slice_in_dim(threshold, first, share, 0)
    update = jnp.clip(votes / own_limits.astype(F32)[None, :], -1.0, 1.0)
    new_weight = (own_columns.astype(F32) - 0.5 * update).astype(BF16)
    return key_values, input_grad, fresh[None], new_weight


def per_device(tokens, cotangent, weight, momentum, threshold):
    depth, width = weight.shape
    n_dp, n_tensor = lax.axis_size("dp"), lax.axis_size("tensor")
    fits = n_tensor == 4 and n_dp in (4, 8) and width % (n_dp * LANES) == 0 and depth % 256 == 0
    chosen = on_line_of_four if fits else in_general
    return chosen(tokens, cotangent, weight, momentum, threshold)


def solution(mesh):
    in_specs = (P("dp", "tensor"), P("dp", None), P("tensor", None), P("dp", "tensor", None), P())
    out_specs = (
        P(("dp", "tensor"), None),
        P("dp", "tensor"),
        P("dp", "tensor", None),
        P("tensor", "dp"),
    )
    return jax.shard_map(
        per_device, mesh=mesh, in_specs=in_specs, out_specs=out_specs, check_vma=False
    )
```

time: 78.4 us -> 41.9 us (0.53)
  other arithmetic: 20.5 us -> 0 us
  between operations: 14.1 us -> 0.71 us
  local copies, waits for them, and re-layouts: 15.1 us -> 3.89 us
  starting transfers between devices: 5.41 us -> 15.2 us
  matrix products: 9.39 us -> 1.9 us
  Pallas kernels: 0 us -> 6.01 us
    ppermute x0 -> x8, starting transfers between devices: none -> 15.2 us  [the longest x4 11.2 us: along(): return lax.ppermute(value, 'tensor', pairs)]
    ppermute x0 -> x8, waiting for transfers between devices: none -> 13.9 us  [the longest x4 13.9 us: along(): return lax.ppermute(value, 'tensor', pairs)]
    all_to_all x1 -> x0, waiting for transfers between devices: 13.5 us -> none  [per_device(): lax.all_to_all(fresh[None], 'dp', split_axis=2, concat_axis=0, tiled=True)]
    unnamed x1 -> x0, other arithmetic: 11.2 us -> none
    dot_general x3 -> x1, matrix products: 9.39 us -> 1.9 us  [on_line_of_four(): lax.dot_general(cotangent, weight, (((1,), (1,)), ((), ())), preferred_el...]
    min x1 -> x0, other arithmetic: 6.23 us -> none  [per_device(): jnp.clip(arrived.astype(jnp.float32) / 0.125, -1.0, 1.0)]
    pallas_call x0 -> x7, Pallas kernels: none -> 6.01 us  [call(): pl.pallas_call(kernel, out_shape=outs, compiler_params=params(), **more)]
    broadcast_in_dim x1 -> x0, local copies, waits for them, and re-layouts: 5.9 us -> none  [per_device(): return (key_values, input_grad, fresh[None], new_weight)]
  transfers between devices with their start and end apart: 2 -> 8, of which waited for: 1 -> 3; matrix products, arithmetic and copies ran while one was open for 29% -> 5% of each run, Pallas kernels for 0% -> 5%
where the time goes in v1:
time: 41.9 us; the launch traced here: 41.7 us
  starting transfers between devices  15.2 us (36%)
  waiting for transfers between devices  13.9 us (33%)
  Pallas kernels  6.01 us (14%)
  local copies, waits for them, and re-layouts  3.89 us (9%)
  matrix products  1.9 us (5%)
  between operations  0.71 us (2%)
    ppermute x4, waiting for transfers between devices, along(): return lax.ppermute(value, 'tensor', pairs)  13.9 us
    ppermute x4, starting transfers between devices, along(): return lax.ppermute(value, 'tensor', pairs)  11.2 us
    pallas_call x7, Pallas kernels, call(): pl.pallas_call(kernel, out_shape=outs, compiler_params=params(), **more)  6.01 us
    ppermute x4, starting transfers between devices, over(): return lax.ppermute(value, 'dp', [(i, i ^ mask) for i in range(n_dp)])  4.05 us
    unnamed x12, local copies, waits for them, and re-layouts  3.89 us
    dot_general x1, matrix products, on_line_of_four(): lax.dot_general(cotangent, weight, (((1,), (1,)), ((), ())), preferred_el...  1.9 us
  transfers between devices with their start and end apart: 8, of which 3 were waited for; matrix products, arithmetic and copies ran while one was open for 5% of the time, Pallas kernels for 5%

profile of v1, /device:TPU:0, one launch (start us, length us, event | category | flops | bytes accessed | tf_op | source)
XLA Modules:
  0.0 41.7 jit_solution(6927740525927883120)
XLA Ops:
  0.6 0.0 copy-start
  0.6 0.0 copy-start.1
  0.7 1.2 %copy-done.1 = bf16[512,768]{1,0:T(8,128)(2,1)S(1)} copy-done((bf16[512,768]{1,0:T(8,128)(2,1)S(1)}, bf16[512,768]{1,0:T(8,128)(2,1)}, u32[]{:S(2)}) %copy-start.1) | copy-done | bytes 786456
  1.9 0.0 copy-start.2
  1.9 1.4 %copy-done.2 = bf16[1,768,1024]{2,1,0:T(8,128)(2,1)S(1)} copy-done((bf16[1,768,1024]{2,1,0:T(8,128)(2,1)S(1)}, bf16[1,768,1024]{2,1,0:T(8,128)(2,1)}, u32[]{:S(2)}) %copy-start.2) | copy-done | bytes 1572888
  3.3 0.0 copy-start.3
  3.3 1.2 %copy-done.3 = bf16[512,1024]{1,0:T(8,128)(2,1)S(1)} copy-done((bf16[512,1024]{1,0:T(8,128)(2,1)S(1)}, bf16[512,1024]{1,0:T(8,128)(2,1)}, u32[]{:S(2)}) %copy-start.3) | copy-done | bytes 1048600
  4.5 3.0 %shard_map.88 = (bf16[1,768,1024]{2,1,0:T(8,128)(2,1)}, bf16[4,768,128]{2,1,0:T(8,128)(2,1)S(1)}, bf16[4,768,128]{2,1,0:T(8,128)(2,1)S(1)}) custom-call(bf16[512,768]{1,0:T(8,128)(2,1)S(1)} %copy-done.1, bf16[512,1024]{1,0:T(8,128)(2,1)S(1)} %copy-done.3, bf16[1,768,1024]{2,1,0:T(8,128)(2,1)S(1)} %copy-done.2), custom_call_target="tpu_custom_call" | custom-call | tf_op jit(solution)/shard_map/pallas_call | solution.py:125
  7.5 0.5 %collective-permute-start.4 = (bf16[4,768,128]{2,1,0:T(8,128)(2,1)S(1)}, bf16[4,768,128]{2,1,0:T(8,128)(2,1)S(1)}, u32[]{:S(2)}, u32[]{:S(2)}) collective-permute-start(bf16[4,768,128]{2,1,0:T(8,128)(2,1)S(1)} %get-tuple-element.19), channel_id=1, source_target_pairs={{0,4},{4,0},{8,12},{12,8},{16,20},{20,16},{24,28},{28,24},{1,5},{5... | collective-permute-start | bytes 2359304 | tf_op jit(solution)/shard_map/ppermute | solution.py:146
  8.0 0.0 copy-done
  8.0 0.4 shard_map.85
  8.4 2.6 %collective-permute-start = (bf16[128,1024]{1,0:T(8,128)(2,1)S(1)}, bf16[128,1024]{1,0:T(8,128)(2,1)S(1)}, u32[]{:S(2)}, u32[]{:S(2)}) collective-permute-start(bf16[128,1024]{1,0:T(8,128)(2,1)S(1)} %shard_map.85), channel_id=1, source_target_pairs={{0,1},{3,2},{1,0},{2,3},{4,5},{7,6},{5,4},{6,7},{8,9},{11,10},{9,8... | collective-permute-start | bytes 786440 | tf_op jit(solution)/shard_map/ppermute | solution.py:143
  11.0 0.8 %shard_map.84 = (bf16[128,1024]{1,0:T(8,128)(2,1)S(1)}, bf16[128,1024]{1,0:T(8,128)(2,1)S(1)}, bf16[128,1024]{1,0:T(8,128)(2,1)S(1)}) custom-call(bf16[512,768]{1,0:T(8,128)(2,1)S(1)} %copy-done.1, bf16[768,1024]{1,0:T(8,128)(2,1)S(1)} %copy-done), custom_call_target="tpu_custom_call" | custom-call | tf_op jit(solution)/shard_map/pallas_call | solution.py:125
  11.8 0.0 copy-start.4
  11.8 0.8 %collective-permute-start.1 = (bf16[128,1024]{1,0:T(8,128)(2,1)S(1)}, bf16[128,1024]{1,0:T(8,128)(2,1)S(1)}, u32[]{:S(2)}, u32[]{:S(2)}) collective-permute-start(bf16[128,1024]{1,0:T(8,128)(2,1)S(1)} %get-tuple-element.15), channel_id=1, source_target_pairs={{1,2},{2,1},{0,0},{3,3},{5,6},{6,5},{4,4},{7,7},{9,10},{10,9},{8,8... | collective-permute-start | bytes 786440 | tf_op jit(solution)/shard_map/ppermute | solution.py:143
  12.7 4.4 %collective-permute-start.2 = (bf16[128,1024]{1,0:T(8,128)(2,1)S(1)}, bf16[128,1024]{1,0:T(8,128)(2,1)S(1)}, u32[]{:S(2)}, u32[]{:S(2)}) collective-permute-start(bf16[128,1024]{1,0:T(8,128)(2,1)S(1)} %get-tuple-element.15), channel_id=1, source_target_pairs={{0,1},{3,2},{1,3},{2,0},{4,5},{7,6},{5,7},{6,4},{8,9},{11,10},{9,1... | collective-permute-start | bytes 786440 | tf_op jit(solution)/shard_map/ppermute | solution.py:143
  17.1 0.9 %collective-permute-done.refs_1_ = bf16[128,1024]{1,0:T(8,128)(2,1)S(1)} collective-permute-done((bf16[128,1024]{1,0:T(8,128)(2,1)S(1)}, bf16[128,1024]{1,0:T(8,128)(2,1)S(1)}, u32[]{:S(2)}, u32[]{:S(2)}) %collective-permute-start) | collective-permute-done | bytes 262176 | tf_op jit(solution)/shard_map/ppermute | solution.py:143
  18.0 3.3 %collective-permute-start.3 = (bf16[128,1024]{1,0:T(8,128)(2,1)S(1)}, bf16[128,1024]{1,0:T(8,128)(2,1)S(1)}, u32[]{:S(2)}, u32[]{:S(2)}) collective-permute-start(bf16[128,1024]{1,0:T(8,128)(2,1)S(1)} %shard_map.86), channel_id=1, source_target_pairs={{0,2},{3,1},{1,3},{2,0},{4,6},{7,5},{5,7},{6,4},{8,10},{11,9},{9,1... | collective-permute-start | bytes 786440 | tf_op jit(solution)/shard_map/ppermute | solution.py:143
  21.4 0.0 collective-permute-done.4.refs_1_
  21.4 0.2 shard_map.89
  21.5 1.6 %collective-permute-start.5 = (bf16[768,128]{1,0:T(8,128)(2,1)S(1)}, bf16[768,128]{1,0:T(8,128)(2,1)S(1)}, u32[]{:S(2)}, u32[]{:S(2)}) collective-permute-start(bf16[768,128]{1,0:T(8,128)(2,1)S(1)} %get-tuple-element.21), channel_id=1, source_target_pairs={{0,8},{4,12},{8,0},{12,4},{16,24},{20,28},{24,16},{28,20},{1,9},{5... | collective-permute-start | bytes 589832 | tf_op jit(solution)/shard_map/ppermute | solution.py:146
  23.1 1.5 %collective-permute-start.6 = (bf16[768,128]{1,0:T(8,128)(2,1)S(1)}, bf16[768,128]{1,0:T(8,128)(2,1)S(1)}, u32[]{:S(2)}, u32[]{:S(2)}) collective-permute-start(bf16[768,128]{1,0:T(8,128)(2,1)S(1)} %get-tuple-element.22), channel_id=1, source_target_pairs={{0,16},{4,20},{8,24},{12,28},{16,0},{20,4},{24,8},{28,12},{1,17},{... | collective-permute-start | bytes 589832 | tf_op jit(solution)/shard_map/ppermute | solution.py:146
  24.6 0.0 collective-permute-done.1.refs_2_
  24.6 0.5 %collective-permute-start.7 = (bf16[768,128]{1,0:T(8,128)(2,1)S(1)}, bf16[768,128]{1,0:T(8,128)(2,1)S(1)}, u32[]{:S(2)}, u32[]{:S(2)}) collective-permute-start(bf16[768,128]{1,0:T(8,128)(2,1)S(1)} %get-tuple-element.23), channel_id=1, source_target_pairs={{0,24},{4,28},{8,16},{12,20},{16,8},{20,12},{24,0},{28,4},{1,25},{... | collective-permute-start | bytes 589832 | tf_op jit(solution)/shard_map/ppermute | solution.py:146
  25.1 0.0 copy-done.4
  25.1 1.9 %multiply_convert_fusion = bf16[512,768]{1,0:T(8,128)(2,1)} fusion(bf16[512,1024]{1,0:T(8,128)(2,1)S(1)} %copy-done.4, bf16[768,1024]{1,0:T(8,128)(2,1)S(1)} %copy-done), kind=kOutput, calls=%fused_computation | convolution fusion | flops 806092800 | bytes 3407872 | tf_op jit(solution)/shard_map/dot_general | solution.py:189
  27.0 0.0 copy-start.5
  27.0 7.8 %collective-permute-done.2.refs_3_ = bf16[128,1024]{1,0:T(8,128)(2,1)S(1)} collective-permute-done((bf16[128,1024]{1,0:T(8,128)(2,1)S(1)}, bf16[128,1024]{1,0:T(8,128)(2,1)S(1)}, u32[]{:S(2)}, u32[]{:S(2)}) %collective-permute-start.2) | collective-permute-done | bytes 262176 | tf_op jit(solution)/shard_map/ppermute | solution.py:143
  34.9 5.2 %collective-permute-done.3.refs_4_ = bf16[128,1024]{1,0:T(8,128)(2,1)S(1)} collective-permute-done((bf16[128,1024]{1,0:T(8,128)(2,1)S(1)}, bf16[128,1024]{1,0:T(8,128)(2,1)S(1)}, u32[]{:S(2)}, u32[]{:S(2)}) %collective-permute-start.3) | collective-permute-done | bytes 262176 | tf_op jit(solution)/shard_map/ppermute | solution.py:143
  40.0 0.8 %shard_map.87 = bf16[128,1024]{1,0:T(8,128)(2,1)} custom-call(bf16[128,1024]{1,0:T(8,128)(2,1)S(1)} %get-tuple-element.14.refs_0_, bf16[128,1024]{1,0:T(8,128)(2,1)S(1)} %collective-permute-done.refs_1_, bf16[128,1024]{1,0:T(8,128)(2,1)S(1)} %collective-permute-done.1.refs_2_, bf16[128,1024]{1,0:T(8,128)(2,1)S(1)} %collective-permute-done.2.refs_3_, ...), custom_call_target="tpu_custom_call" | custom-call | tf_op jit(solution)/shard_map/pallas_call | solution.py:125
  40.8 0.0 collective-permute-done.5.refs_3_
  40.8 0.0 collective-permute-done.6.refs_4_
  40.8 0.0 collective-permute-done.7.refs_5_
  40.8 0.0 copy-done.5
  40.8 0.8 %shard_map.90 = bf16[768,128]{1,0:T(8,128)(2,1)} custom-call(bf16[768,1024]{1,0:T(8,128)(2,1)S(1)} %copy-done, s32[1,1024]{1,0:T(1,128)S(1)} %bitcast.3, bf16[768,128]{1,0:T(8,128)(2,1)S(1)} %get-tuple-element.20.refs_2_, bf16[768,128]{1,0:T(8,128)(2,1)S(1)} %collective-permute-done.5.refs_3_, bf16[768,128]{1,0:T(8,128)(2,1)S(1)} %collective-permute-done.6.refs_4_, ...), custom_call_target="tpu_custom_call" | custom-call | tf_op jit(solution)/shard_map/pallas_call | solution.py:125
  (1 shorter events, 0.0 us)
Async XLA Ops:
  0.6 7.4 %copy-start = (bf16[768,1024]{1,0:T(8,128)(2,1)S(1)}, bf16[768,1024]{1,0:T(8,128)(2,1)}, u32[]{:S(2)}) copy-start(bf16[768,1024]{1,0:T(8,128)(2,1)} %refs_0_.7) | copy-start | bytes 4718596
  0.6 1.3 %copy-start.1 = (bf16[512,768]{1,0:T(8,128)(2,1)S(1)}, bf16[512,768]{1,0:T(8,128)(2,1)}, u32[]{:S(2)}) copy-start(bf16[512,768]{1,0:T(8,128)(2,1)} %refs_0_.6) | copy-start | bytes 2359300
  1.9 1.4 %copy-start.2 = (bf16[1,768,1024]{2,1,0:T(8,128)(2,1)S(1)}, bf16[1,768,1024]{2,1,0:T(8,128)(2,1)}, u32[]{:S(2)}) copy-start(bf16[1,768,1024]{2,1,0:T(8,128)(2,1)} %refs_2_.1) | copy-start | bytes 4718596
  3.3 1.2 %copy-start.3 = (bf16[512,1024]{1,0:T(8,128)(2,1)S(1)}, bf16[512,1024]{1,0:T(8,128)(2,1)}, u32[]{:S(2)}) copy-start(bf16[512,1024]{1,0:T(8,128)(2,1)} %refs_1_.5) | copy-start | bytes 3145732
  7.5 13.8 %collective-permute-start.4 = (bf16[4,768,128]{2,1,0:T(8,128)(2,1)S(1)}, bf16[4,768,128]{2,1,0:T(8,128)(2,1)S(1)}, u32[]{:S(2)}, u32[]{:S(2)}) collective-permute-start(bf16[4,768,128]{2,1,0:T(8,128)(2,1)S(1)} %get-tuple-element.19), channel_id=1, source_target_pairs={{0,4},{4,0},{8,12},{12,8},{16,20},{20,16},{24,28},{28,24},{1,5},{5... | collective-permute-start | bytes 2359304 | tf_op jit(solution)/shard_map/ppermute | solution.py:146
  8.4 9.6 %collective-permute-start = (bf16[128,1024]{1,0:T(8,128)(2,1)S(1)}, bf16[128,1024]{1,0:T(8,128)(2,1)S(1)}, u32[]{:S(2)}, u32[]{:S(2)}) collective-permute-start(bf16[128,1024]{1,0:T(8,128)(2,1)S(1)} %shard_map.85), channel_id=1, source_target_pairs={{0,1},{3,2},{1,0},{2,3},{4,5},{7,6},{5,4},{6,7},{8,9},{11,10},{9,8... | collective-permute-start | bytes 786440 | tf_op jit(solution)/shard_map/ppermute | solution.py:143
  11.8 13.3 %copy-start.4 = (bf16[512,1024]{1,0:T(8,128)(2,1)S(1)}, bf16[512,1024]{1,0:T(8,128)(2,1)}, u32[]{:S(2)}) copy-start(bf16[512,1024]{1,0:T(8,128)(2,1)} %refs_1_.5) | copy-start | bytes 3145732
  11.8 12.8 %collective-permute-start.1 = (bf16[128,1024]{1,0:T(8,128)(2,1)S(1)}, bf16[128,1024]{1,0:T(8,128)(2,1)S(1)}, u32[]{:S(2)}, u32[]{:S(2)}) collective-permute-start(bf16[128,1024]{1,0:T(8,128)(2,1)S(1)} %get-tuple-element.15), channel_id=1, source_target_pairs={{1,2},{2,1},{0,0},{3,3},{5,6},{6,5},{4,4},{7,7},{9,10},{10,9},{8,8... | collective-permute-start | bytes 786440 | tf_op jit(solution)/shard_map/ppermute | solution.py:143
  12.7 22.2 %collective-permute-start.2 = (bf16[128,1024]{1,0:T(8,128)(2,1)S(1)}, bf16[128,1024]{1,0:T(8,128)(2,1)S(1)}, u32[]{:S(2)}, u32[]{:S(2)}) collective-permute-start(bf16[128,1024]{1,0:T(8,128)(2,1)S(1)} %get-tuple-element.15), channel_id=1, source_target_pairs={{0,1},{3,2},{1,3},{2,0},{4,5},{7,6},{5,7},{6,4},{8,9},{11,10},{9,1... | collective-permute-start | bytes 786440 | tf_op jit(solution)/shard_map/ppermute | solution.py:143
  18.0 22.0 %collective-permute-start.3 = (bf16[128,1024]{1,0:T(8,128)(2,1)S(1)}, bf16[128,1024]{1,0:T(8,128)(2,1)S(1)}, u32[]{:S(2)}, u32[]{:S(2)}) collective-permute-start(bf16[128,1024]{1,0:T(8,128)(2,1)S(1)} %shard_map.86), channel_id=1, source_target_pairs={{0,2},{3,1},{1,3},{2,0},{4,6},{7,5},{5,7},{6,4},{8,10},{11,9},{9,1... | collective-permute-start | bytes 786440 | tf_op jit(solution)/shard_map/ppermute | solution.py:143
  21.5 19.3 %collective-permute-start.5 = (bf16[768,128]{1,0:T(8,128)(2,1)S(1)}, bf16[768,128]{1,0:T(8,128)(2,1)S(1)}, u32[]{:S(2)}, u32[]{:S(2)}) collective-permute-start(bf16[768,128]{1,0:T(8,128)(2,1)S(1)} %get-tuple-element.21), channel_id=1, source_target_pairs={{0,8},{4,12},{8,0},{12,4},{16,24},{20,28},{24,16},{28,20},{1,9},{5... | collective-permute-start | bytes 589832 | tf_op jit(solution)/shard_map/ppermute | solution.py:146
  23.1 17.7 %collective-permute-start.6 = (bf16[768,128]{1,0:T(8,128)(2,1)S(1)}, bf16[768,128]{1,0:T(8,128)(2,1)S(1)}, u32[]{:S(2)}, u32[]{:S(2)}) collective-permute-start(bf16[768,128]{1,0:T(8,128)(2,1)S(1)} %get-tuple-element.22), channel_id=1, source_target_pairs={{0,16},{4,20},{8,24},{12,28},{16,0},{20,4},{24,8},{28,12},{1,17},{... | collective-permute-start | bytes 589832 | tf_op jit(solution)/shard_map/ppermute | solution.py:146
  24.6 16.2 %collective-permute-start.7 = (bf16[768,128]{1,0:T(8,128)(2,1)S(1)}, bf16[768,128]{1,0:T(8,128)(2,1)S(1)}, u32[]{:S(2)}, u32[]{:S(2)}) collective-permute-start(bf16[768,128]{1,0:T(8,128)(2,1)S(1)} %get-tuple-element.23), channel_id=1, source_target_pairs={{0,24},{4,28},{8,16},{12,20},{16,8},{20,12},{24,0},{28,4},{1,25},{... | collective-permute-start | bytes 589832 | tf_op jit(solution)/shard_map/ppermute | solution.py:146
  27.0 13.8 %copy-start.5 = (s32[1024]{0:T(1024)S(1)}, s32[1024]{0:T(1024)}, u32[]{:S(2)}) copy-start(s32[1024]{0:T(1024)} %param.9) | copy-start | bytes 12292

commit v2 on v1

--- a/solution.py
+++ b/solution.py
@@ -4,6 +4,7 @@
 from jax.experimental import pallas as pl
 from jax.experimental.pallas import tpu as pltpu
 from jax.sharding import PartitionSpec as P
+
 
 BF16 = jnp.bfloat16
 F32 = jnp.float32
@@ -120,6 +121,10 @@
 
 
 def call(kernel, outs, *args, **more):
+    return run_kernel(kernel, outs, *args, **more)
+
+
+def run_kernel(kernel, outs, *args, **more):
     more.setdefault("in_specs", [WHOLE] * len(args))
     more.setdefault("out_specs", [WHOLE] * len(outs))
     return pl.pallas_call(kernel, out_shape=outs, compiler_params=params(), **more)(*args)
@@ -149,8 +154,7 @@
     seed_came = along(seed, (0, 1), (3, 2), (1, 0), (2, 3))
 
     tile = 256
-    fresh, send, keep = call(
-        bind(momentum_kernel, inverse, share),
+    fresh, send, keep = call(bind(momentum_kernel, inverse, share),
         [
             shaped(1, depth, width),
             shaped(n_dp // 2, depth, share),
@@ -173,32 +177,30 @@
     )
     came = over(send, 1)
 
-    near, third, own = call(
-        bind(rest_kernel, inverse, rows), [shaped(rows, width)] * 3, tokens, weight
-    )
-    near_came = along(near, (0, 1), (3, 2), (1, 3), (2, 0))
+    near, third, own = call(bind(rest_kernel, inverse, rows), [shaped(rows, width)] * 3, tokens, weight
+    )
+    near_came = along(near, (0, 1), (3, 2))
     across_came = along(near, (1, 2), (2, 1), (0, 0), (3, 3))
 
     sums = call(bind(pair_kernel), [shaped(depth, share)] * (n_dp // 2), keep, came)
-    votes = [sums[0]] + [over(sums[k], 2 * k) for k in range(1, n_dp // 2)]
+    farther = {k: over(sums[k], 2 * k) for k in reversed(range(1, n_dp // 2))}
+    votes = [sums[0]] + [farther[k] for k in range(1, n_dp // 2)]
 
     (relay,) = call(bind(relay_kernel), [shaped(rows, width)], third, seed_came)
     third_came = along(relay, (0, 2), (3, 1), (1, 3), (2, 0))
 
-    input_grad = (
-        lax.dot_general(cotangent, weight, (((1,), (1,)), ((), ())), preferred_element_type=F32)
-        * inverse
-    ).astype(BF16)
-
-    (new_weight,) = call(
-        bind(weight_kernel, share),
+    input_grad = lax.dot_general(
+        cotangent, weight, (((1,), (1,)), ((), ())), preferred_element_type=F32
+    )
+    input_grad = (input_grad * inverse).astype(BF16)
+
+    (new_weight,) = call(bind(weight_kernel, share),
         [shaped(depth, share)],
         weight,
         threshold.reshape(1, width),
         *votes,
     )
-    (key_values,) = call(
-        bind(keys_kernel), [shaped(rows, width)], own, seed_came, across_came, near_came, third_came
+    (key_values,) = call(bind(keys_kernel), [shaped(rows, width)], own, seed_came, across_came, near_came, third_came
     )
     return key_values, input_grad, fresh, new_weight
 

time: 41.9 us -> 36.3 us (0.87)
  waiting for transfers between devices: 13.9 us -> 7.87 us
  starting transfers between devices: 15.2 us -> 15.7 us
    ppermute x4, waiting for transfers between devices: 13.9 us -> 7.86 us  [along(): return lax.ppermute(value, 'tensor', pairs)]
    ppermute x4, starting transfers between devices: 11.2 us -> 11.6 us  [along(): return lax.ppermute(value, 'tensor', pairs)]
  transfers between devices with their start and end apart: 8 -> 8, of which waited for: 3 -> 1; matrix products, arithmetic and copies ran while one was open for 5% -> 5% of each run, Pallas kernels for 5% -> 6%
where the time goes in v2:
time: 36.3 us; the launch traced here: 36.1 us
  starting transfers between devices  15.7 us (43%)
  waiting for transfers between devices  7.87 us (22%)
  Pallas kernels  6.03 us (17%)
  local copies, waits for them, and re-layouts  3.89 us (11%)
  matrix products  1.9 us (5%)
  between operations  0.72 us (2%)
    ppermute x4, starting transfers between devices, along(): return lax.ppermute(value, 'tensor', pairs)  11.6 us
    ppermute x4, waiting for transfers between devices, along(): return lax.ppermute(value, 'tensor', pairs)  7.86 us
    pallas_call x7, Pallas kernels, run_kernel(): pl.pallas_call(kernel, out_shape=outs, compiler_params=params(), **more)  6.03 us
    ppermute x4, starting transfers between devices, over(): return lax.ppermute(value, 'dp', [(i, i ^ mask) for i in range(n_dp)])  4.05 us
    unnamed x12, local copies, waits for them, and re-layouts  3.89 us
    dot_general x1, matrix products, on_line_of_four(): lax.dot_general(cotangent, weight, (((1,), (1,)), ((), ())), preferred_el...  1.9 us
  transfers between devices with their start and end apart: 8, of which 1 were waited for; matrix products, arithmetic and copies ran while one was open for 5% of the time, Pallas kernels for 6%

profile of v2, /device:TPU:0, one launch (start us, length us, event | category | flops | bytes accessed | tf_op | source)
XLA Modules:
  0.0 36.1 jit_solution(14759041316748994136)
XLA Ops:
  0.6 0.0 copy-start
  0.6 0.0 copy-start.1
  0.7 1.2 %copy-done.1 = bf16[512,768]{1,0:T(8,128)(2,1)S(1)} copy-done((bf16[512,768]{1,0:T(8,128)(2,1)S(1)}, bf16[512,768]{1,0:T(8,128)(2,1)}, u32[]{:S(2)}) %copy-start.1) | copy-done | bytes 786456
  1.9 0.0 copy-start.2
  1.9 1.4 %copy-done.2 = bf16[1,768,1024]{2,1,0:T(8,128)(2,1)S(1)} copy-done((bf16[1,768,1024]{2,1,0:T(8,128)(2,1)S(1)}, bf16[1,768,1024]{2,1,0:T(8,128)(2,1)}, u32[]{:S(2)}) %copy-start.2) | copy-done | bytes 1572888
  3.3 0.0 copy-start.3
  3.3 1.2 %copy-done.3 = bf16[512,1024]{1,0:T(8,128)(2,1)S(1)} copy-done((bf16[512,1024]{1,0:T(8,128)(2,1)S(1)}, bf16[512,1024]{1,0:T(8,128)(2,1)}, u32[]{:S(2)}) %copy-start.3) | copy-done | bytes 1048600
  4.5 3.0 %shard_map.88 = (bf16[1,768,1024]{2,1,0:T(8,128)(2,1)}, bf16[4,768,128]{2,1,0:T(8,128)(2,1)S(1)}, bf16[4,768,128]{2,1,0:T(8,128)(2,1)S(1)}) custom-call(bf16[512,768]{1,0:T(8,128)(2,1)S(1)} %copy-done.1, bf16[512,1024]{1,0:T(8,128)(2,1)S(1)} %copy-done.3, bf16[1,768,1024]{2,1,0:T(8,128)(2,1)S(1)} %copy-done.2), custom_call_target="tpu_custom_call" | custom-call | tf_op jit(solution)/shard_map/pallas_call | solution.py:130
  7.5 0.5 %collective-permute-start.4 = (bf16[4,768,128]{2,1,0:T(8,128)(2,1)S(1)}, bf16[4,768,128]{2,1,0:T(8,128)(2,1)S(1)}, u32[]{:S(2)}, u32[]{:S(2)}) collective-permute-start(bf16[4,768,128]{2,1,0:T(8,128)(2,1)S(1)} %get-tuple-element.19), channel_id=1, source_target_pairs={{0,4},{4,0},{8,12},{12,8},{16,20},{20,16},{24,28},{28,24},{1,5},{5... | collective-permute-start | bytes 2359304 | tf_op jit(solution)/shard_map/ppermute | solution.py:151
  8.0 0.0 copy-done
  8.0 0.4 %shard_map.85 = bf16[128,1024]{1,0:T(8,128)(2,1)S(1)} custom-call(bf16[512,768]{1,0:T(8,128)(2,1)S(1)} %copy-done.1, bf16[768,1024]{1,0:T(8,128)(2,1)S(1)} %copy-done), custom_call_target="tpu_custom_call" | custom-call | tf_op jit(solution)/shard_map/pallas_call | solution.py:130
  8.4 2.6 %collective-permute-start = (bf16[128,1024]{1,0:T(8,128)(2,1)S(1)}, bf16[128,1024]{1,0:T(8,128)(2,1)S(1)}, u32[]{:S(2)}, u32[]{:S(2)}) collective-permute-start(bf16[128,1024]{1,0:T(8,128)(2,1)S(1)} %shard_map.85), channel_id=1, source_target_pairs={{0,1},{3,2},{1,0},{2,3},{4,5},{7,6},{5,4},{6,7},{8,9},{11,10},{9,8... | collective-permute-start | bytes 786440 | tf_op jit(solution)/shard_map/ppermute | solution.py:148
  11.0 0.8 %shard_map.84 = (bf16[128,1024]{1,0:T(8,128)(2,1)S(1)}, bf16[128,1024]{1,0:T(8,128)(2,1)S(1)}, bf16[128,1024]{1,0:T(8,128)(2,1)S(1)}) custom-call(bf16[512,768]{1,0:T(8,128)(2,1)S(1)} %copy-done.1, bf16[768,1024]{1,0:T(8,128)(2,1)S(1)} %copy-done), custom_call_target="tpu_custom_call" | custom-call | tf_op jit(solution)/shard_map/pallas_call | solution.py:130
  11.8 0.0 copy-start.4
  11.8 0.8 %collective-permute-start.1 = (bf16[128,1024]{1,0:T(8,128)(2,1)S(1)}, bf16[128,1024]{1,0:T(8,128)(2,1)S(1)}, u32[]{:S(2)}, u32[]{:S(2)}) collective-permute-start(bf16[128,1024]{1,0:T(8,128)(2,1)S(1)} %get-tuple-element.15), channel_id=1, source_target_pairs={{1,2},{2,1},{0,0},{3,3},{5,6},{6,5},{4,4},{7,7},{9,10},{10,9},{8,8... | collective-permute-start | bytes 786440 | tf_op jit(solution)/shard_map/ppermute | solution.py:148
  12.7 6.3 %collective-permute-start.2 = (bf16[128,1024]{1,0:T(8,128)(2,1)S(1)}, bf16[128,1024]{1,0:T(8,128)(2,1)S(1)}, u32[]{:S(2)}, u32[]{:S(2)}) collective-permute-start(bf16[128,1024]{1,0:T(8,128)(2,1)S(1)} %get-tuple-element.15), channel_id=1, source_target_pairs={{0,1},{3,2},{4,5},{7,6},{8,9},{11,10},{12,13},{15,14},{16,17},{19,... | collective-permute-start | bytes 786440 | tf_op jit(solution)/shard_map/ppermute | solution.py:148
  19.0 0.0 collective-permute-done.refs_1_
  19.0 1.9 %collective-permute-start.3 = (bf16[128,1024]{1,0:T(8,128)(2,1)S(1)}, bf16[128,1024]{1,0:T(8,128)(2,1)S(1)}, u32[]{:S(2)}, u32[]{:S(2)}) collective-permute-start(bf16[128,1024]{1,0:T(8,128)(2,1)S(1)} %shard_map.86), channel_id=1, source_target_pairs={{0,2},{3,1},{1,3},{2,0},{4,6},{7,5},{5,7},{6,4},{8,10},{11,9},{9,1... | collective-permute-start | bytes 786440 | tf_op jit(solution)/shard_map/ppermute | solution.py:148
  20.9 0.0 collective-permute-done.4.refs_1_
  20.9 0.2 shard_map.89
  21.1 1.6 %collective-permute-start.5 = (bf16[768,128]{1,0:T(8,128)(2,1)S(1)}, bf16[768,128]{1,0:T(8,128)(2,1)S(1)}, u32[]{:S(2)}, u32[]{:S(2)}) collective-permute-start(bf16[768,128]{1,0:T(8,128)(2,1)S(1)} %get-tuple-element.21), channel_id=1, source_target_pairs={{0,8},{4,12},{8,0},{12,4},{16,24},{20,28},{24,16},{28,20},{1,9},{5... | collective-permute-start | bytes 589832 | tf_op jit(solution)/shard_map/ppermute | solution.py:151
  22.6 1.5 %collective-permute-start.6 = (bf16[768,128]{1,0:T(8,128)(2,1)S(1)}, bf16[768,128]{1,0:T(8,128)(2,1)S(1)}, u32[]{:S(2)}, u32[]{:S(2)}) collective-permute-start(bf16[768,128]{1,0:T(8,128)(2,1)S(1)} %get-tuple-element.22), channel_id=1, source_target_pairs={{0,16},{4,20},{8,24},{12,28},{16,0},{20,4},{24,8},{28,12},{1,17},{... | collective-permute-start | bytes 589832 | tf_op jit(solution)/shard_map/ppermute | solution.py:151
  24.2 0.0 collective-permute-done.1.refs_2_
  24.2 0.5 %collective-permute-start.7 = (bf16[768,128]{1,0:T(8,128)(2,1)S(1)}, bf16[768,128]{1,0:T(8,128)(2,1)S(1)}, u32[]{:S(2)}, u32[]{:S(2)}) collective-permute-start(bf16[768,128]{1,0:T(8,128)(2,1)S(1)} %get-tuple-element.23), channel_id=1, source_target_pairs={{0,24},{4,28},{8,16},{12,20},{16,8},{20,12},{24,0},{28,4},{1,25},{... | collective-permute-start | bytes 589832 | tf_op jit(solution)/shard_map/ppermute | solution.py:151
  24.6 0.0 copy-done.4
  24.6 1.9 %multiply_convert_fusion = bf16[512,768]{1,0:T(8,128)(2,1)} fusion(bf16[512,1024]{1,0:T(8,128)(2,1)S(1)} %copy-done.4, bf16[768,1024]{1,0:T(8,128)(2,1)S(1)} %copy-done), kind=kOutput, calls=%fused_computation | convolution fusion | flops 806092800 | bytes 3407872 | tf_op jit(solution)/shard_map/dot_general | solution.py:192
  26.5 0.0 copy-start.5
  26.5 0.0 collective-permute-done.2.refs_3_
  26.5 7.9 %collective-permute-done.3.refs_4_ = bf16[128,1024]{1,0:T(8,128)(2,1)S(1)} collective-permute-done((bf16[128,1024]{1,0:T(8,128)(2,1)S(1)}, bf16[128,1024]{1,0:T(8,128)(2,1)S(1)}, u32[]{:S(2)}, u32[]{:S(2)}) %collective-permute-start.3) | collective-permute-done | bytes 262176 | tf_op jit(solution)/shard_map/ppermute | solution.py:148
  34.4 0.8 %shard_map.87 = bf16[128,1024]{1,0:T(8,128)(2,1)} custom-call(bf16[128,1024]{1,0:T(8,128)(2,1)S(1)} %get-tuple-element.14.refs_0_, bf16[128,1024]{1,0:T(8,128)(2,1)S(1)} %collective-permute-done.refs_1_, bf16[128,1024]{1,0:T(8,128)(2,1)S(1)} %collective-permute-done.1.refs_2_, bf16[128,1024]{1,0:T(8,128)(2,1)S(1)} %collective-permute-done.2.refs_3_, ...), custom_call_target="tpu_custom_call" | custom-call | tf_op jit(solution)/shard_map/pallas_call | solution.py:130
  35.2 0.0 collective-permute-done.5.refs_3_
  35.2 0.0 collective-permute-done.6.refs_4_
  35.2 0.0 collective-permute-done.7.refs_5_
  35.2 0.0 copy-done.5
  35.2 0.8 %shard_map.90 = bf16[768,128]{1,0:T(8,128)(2,1)} custom-call(bf16[768,1024]{1,0:T(8,128)(2,1)S(1)} %copy-done, s32[1,1024]{1,0:T(1,128)S(1)} %bitcast.3, bf16[768,128]{1,0:T(8,128)(2,1)S(1)} %get-tuple-element.20.refs_2_, bf16[768,128]{1,0:T(8,128)(2,1)S(1)} %collective-permute-done.5.refs_3_, bf16[768,128]{1,0:T(8,128)(2,1)S(1)} %collective-permute-done.6.refs_4_, ...), custom_call_target="tpu_custom_call" | custom-call | tf_op jit(solution)/shard_map/pallas_call | solution.py:130
  (1 shorter events, 0.0 us)
Async XLA Ops:
  0.6 7.4 %copy-start = (bf16[768,1024]{1,0:T(8,128)(2,1)S(1)}, bf16[768,1024]{1,0:T(8,128)(2,1)}, u32[]{:S(2)}) copy-start(bf16[768,1024]{1,0:T(8,128)(2,1)} %refs_0_.7) | copy-start | bytes 4718596
  0.6 1.3 %copy-start.1 = (bf16[512,768]{1,0:T(8,128)(2,1)S(1)}, bf16[512,768]{1,0:T(8,128)(2,1)}, u32[]{:S(2)}) copy-start(bf16[512,768]{1,0:T(8,128)(2,1)} %refs_0_.6) | copy-start | bytes 2359300
  1.9 1.4 %copy-start.2 = (bf16[1,768,1024]{2,1,0:T(8,128)(2,1)S(1)}, bf16[1,768,1024]{2,1,0:T(8,128)(2,1)}, u32[]{:S(2)}) copy-start(bf16[1,768,1024]{2,1,0:T(8,128)(2,1)} %refs_2_.1) | copy-start | bytes 4718596
  3.3 1.2 %copy-start.3 = (bf16[512,1024]{1,0:T(8,128)(2,1)S(1)}, bf16[512,1024]{1,0:T(8,128)(2,1)}, u32[]{:S(2)}) copy-start(bf16[512,1024]{1,0:T(8,128)(2,1)} %refs_1_.5) | copy-start | bytes 3145732
  7.5 13.4 %collective-permute-start.4 = (bf16[4,768,128]{2,1,0:T(8,128)(2,1)S(1)}, bf16[4,768,128]{2,1,0:T(8,128)(2,1)S(1)}, u32[]{:S(2)}, u32[]{:S(2)}) collective-permute-start(bf16[4,768,128]{2,1,0:T(8,128)(2,1)S(1)} %get-tuple-element.19), channel_id=1, source_target_pairs={{0,4},{4,0},{8,12},{12,8},{16,20},{20,16},{24,28},{28,24},{1,5},{5... | collective-permute-start | bytes 2359304 | tf_op jit(solution)/shard_map/ppermute | solution.py:151
  8.4 10.6 %collective-permute-start = (bf16[128,1024]{1,0:T(8,128)(2,1)S(1)}, bf16[128,1024]{1,0:T(8,128)(2,1)S(1)}, u32[]{:S(2)}, u32[]{:S(2)}) collective-permute-start(bf16[128,1024]{1,0:T(8,128)(2,1)S(1)} %shard_map.85), channel_id=1, source_target_pairs={{0,1},{3,2},{1,0},{2,3},{4,5},{7,6},{5,4},{6,7},{8,9},{11,10},{9,8... | collective-permute-start | bytes 786440 | tf_op jit(solution)/shard_map/ppermute | solution.py:148
  11.8 12.8 %copy-start.4 = (bf16[512,1024]{1,0:T(8,128)(2,1)S(1)}, bf16[512,1024]{1,0:T(8,128)(2,1)}, u32[]{:S(2)}) copy-start(bf16[512,1024]{1,0:T(8,128)(2,1)} %refs_1_.5) | copy-start | bytes 3145732
  11.8 12.3 %collective-permute-start.1 = (bf16[128,1024]{1,0:T(8,128)(2,1)S(1)}, bf16[128,1024]{1,0:T(8,128)(2,1)S(1)}, u32[]{:S(2)}, u32[]{:S(2)}) collective-permute-start(bf16[128,1024]{1,0:T(8,128)(2,1)S(1)} %get-tuple-element.15), channel_id=1, source_target_pairs={{1,2},{2,1},{0,0},{3,3},{5,6},{6,5},{4,4},{7,7},{9,10},{10,9},{8,8... | collective-permute-start | bytes 786440 | tf_op jit(solution)/shard_map/ppermute | solution.py:148
  12.7 13.9 %collective-permute-start.2 = (bf16[128,1024]{1,0:T(8,128)(2,1)S(1)}, bf16[128,1024]{1,0:T(8,128)(2,1)S(1)}, u32[]{:S(2)}, u32[]{:S(2)}) collective-permute-start(bf16[128,1024]{1,0:T(8,128)(2,1)S(1)} %get-tuple-element.15), channel_id=1, source_target_pairs={{0,1},{3,2},{4,5},{7,6},{8,9},{11,10},{12,13},{15,14},{16,17},{19,... | collective-permute-start | bytes 786440 | tf_op jit(solution)/shard_map/ppermute | solution.py:148
  19.0 15.4 %collective-permute-start.3 = (bf16[128,1024]{1,0:T(8,128)(2,1)S(1)}, bf16[128,1024]{1,0:T(8,128)(2,1)S(1)}, u32[]{:S(2)}, u32[]{:S(2)}) collective-permute-start(bf16[128,1024]{1,0:T(8,128)(2,1)S(1)} %shard_map.86), channel_id=1, source_target_pairs={{0,2},{3,1},{1,3},{2,0},{4,6},{7,5},{5,7},{6,4},{8,10},{11,9},{9,1... | collective-permute-start | bytes 786440 | tf_op jit(solution)/shard_map/ppermute | solution.py:148
  21.1 14.1 %collective-permute-start.5 = (bf16[768,128]{1,0:T(8,128)(2,1)S(1)}, bf16[768,128]{1,0:T(8,128)(2,1)S(1)}, u32[]{:S(2)}, u32[]{:S(2)}) collective-permute-start(bf16[768,128]{1,0:T(8,128)(2,1)S(1)} %get-tuple-element.21), channel_id=1, source_target_pairs={{0,8},{4,12},{8,0},{12,4},{16,24},{20,28},{24,16},{28,20},{1,9},{5... | collective-permute-start | bytes 589832 | tf_op jit(solution)/shard_map/ppermute | solution.py:151
  22.6 12.6 %collective-permute-start.6 = (bf16[768,128]{1,0:T(8,128)(2,1)S(1)}, bf16[768,128]{1,0:T(8,128)(2,1)S(1)}, u32[]{:S(2)}, u32[]{:S(2)}) collective-permute-start(bf16[768,128]{1,0:T(8,128)(2,1)S(1)} %get-tuple-element.22), channel_id=1, source_target_pairs={{0,16},{4,20},{8,24},{12,28},{16,0},{20,4},{24,8},{28,12},{1,17},{... | collective-permute-start | bytes 589832 | tf_op jit(solution)/shard_map/ppermute | solution.py:151
  24.2 11.0 %collective-permute-start.7 = (bf16[768,128]{1,0:T(8,128)(2,1)S(1)}, bf16[768,128]{1,0:T(8,128)(2,1)S(1)}, u32[]{:S(2)}, u32[]{:S(2)}) collective-permute-start(bf16[768,128]{1,0:T(8,128)(2,1)S(1)} %get-tuple-element.23), channel_id=1, source_target_pairs={{0,24},{4,28},{8,16},{12,20},{16,8},{20,12},{24,0},{28,4},{1,25},{... | collective-permute-start | bytes 589832 | tf_op jit(solution)/shard_map/ppermute | solution.py:151
  26.5 8.7 %copy-start.5 = (s32[1024]{0:T(1024)S(1)}, s32[1024]{0:T(1024)}, u32[]{:S(2)}) copy-start(s32[1024]{0:T(1024)} %param.9) | copy-start | bytes 12292

commit v3 on v0

v3 whole, which is shorter than its diff:
```python
import jax
import jax.numpy as jnp
from jax import lax
from jax.experimental import pallas as pl
from jax.experimental.pallas import tpu as pltpu
from jax.sharding import PartitionSpec as P


BF16 = jnp.bfloat16
F32 = jnp.float32
VMEM_LIMIT = 20 * 1024 * 1024
LANES = 128
TILE = 256
IN_VMEM = pl.BlockSpec(memory_space=pltpu.VMEM)
IN_HBM = pl.BlockSpec(memory_space=pltpu.HBM)


def shaped(*dims):
    return jax.ShapeDtypeStruct(dims, BF16)


def seed_block(plane):
    return jnp.where(plane % 2 == 0, 3, 0)


def near_block(plane):
    return jnp.where(plane % 2 == 0, 1, 2)


def third_block(plane):
    return jnp.where(plane == 0, 2, jnp.where(plane == 1, 3, jnp.where(plane == 2, 0, 1)))


def is_outer(plane):
    return jnp.logical_or(plane == 0, plane == 3)


def first_kernel(
    inverse,
    rows,
    tokens,
    weight,
    cotangent,
    seed_ref,
    near_ref,
    tokens_ref,
    weight_ref,
    cot_ref,
    sems,
):
    plane = lax.axis_index("tensor")
    blocks = (seed_block(plane), near_block(plane), third_block(plane), plane)
    spans = [pl.ds(pl.multiple_of(block * rows, rows), rows) for block in blocks]
    tiles = [pl.ds(k * TILE, TILE) for k in range(weight.shape[0] // TILE)]
    moves = [(tokens, tokens_ref, span) for span in spans[:2]]
    moves += [(weight, weight_ref, tile) for tile in tiles]
    moves += [(tokens, tokens_ref, span) for span in spans[2:]]
    moves += [(cotangent, cot_ref, pl.ds(0, cotangent.shape[0]))]
    copies = [
        pltpu.make_async_copy(source.at[span], goal.at[span], sems.at[k])
        for k, (source, goal, span) in enumerate(moves)
    ]
    for copy in copies:
        copy.start()
    copies[0].wait()
    copies[1].wait()
    held = jnp.concatenate([tokens_ref[spans[0], :], tokens_ref[spans[1], :]], axis=0)
    total = None
    for k in range(len(tiles)):
        copies[2 + k].wait()
        part = jnp.dot(
            held[:, k * TILE : (k + 1) * TILE],
            weight_ref[k * TILE : (k + 1) * TILE, :],
            preferred_element_type=F32,
        )
        total = part if total is None else total + part
    result = (total * inverse).astype(BF16)
    seed_ref[...] = result[:rows]
    near_ref[...] = result[rows:]
    for copy in copies[2 + len(tiles) :]:
        copy.wait()


def product_rows(tokens_ref, weight_ref, block, rows, inverse):
    picked = tokens_ref[pl.ds(pl.multiple_of(block * rows, rows), rows), :]
    total = jnp.dot(picked, weight_ref[...], preferred_element_type=F32)
    return (total * inverse).astype(BF16)


def rest_kernel(inverse, rows, tokens_ref, weight_ref, third_ref, own_ref):
    plane = lax.axis_index("tensor")
    third_ref[...] = product_rows(tokens_ref, weight_ref, third_block(plane), rows, inverse)
    own_ref[...] = product_rows(tokens_ref, weight_ref, plane, rows, inverse)


def relay_kernel(third_ref, near_ref, seed_ref, out_ref):
    outer = is_outer(lax.axis_index("tensor"))

    @pl.when(outer)
    def _():
        out_ref[...] = near_ref[...]

    @pl.when(jnp.logical_not(outer))
    def _():
        out_ref[...] = (third_ref[...].astype(F32) + seed_ref[...].astype(F32)).astype(BF16)


def momentum_kernel(step, share, tokens_ref, cot_ref, old_ref, fresh_ref, send_ref, keep_ref):
    odd = lax.axis_index("dp") % 2 == 1
    depth, width = fresh_ref.shape
    for k in range(depth // TILE):
        rows = slice(k * TILE, (k + 1) * TILE)
        turned = tokens_ref[:, rows].T
        for pair in range(width // (2 * share)):
            span = slice(2 * pair * share, 2 * (pair + 1) * share)
            gradient = jnp.dot(turned, cot_ref[:, span], preferred_element_type=F32)
            fresh = (0.9 * old_ref[0, rows, span].astype(F32) + step * gradient).astype(BF16)
            fresh_ref[rows, span] = fresh
            votes = jnp.clip(fresh * BF16(8), BF16(-1), BF16(1))
            low, high = votes[:, :share], votes[:, share:]
            send_ref[pair, rows] = jnp.where(odd, low, high)
            keep_ref[pair, rows] = jnp.where(odd, high, low)


def back_kernel(inverse, cot_ref, weight_ref, fresh_ref, back, new, back_ref, sems):
    store = pltpu.make_async_copy(fresh_ref, new.at[0], sems.at[0])
    store.start()
    rows = cot_ref.shape[0] // 2
    stores = [store]
    for k in range(2):
        span = pl.ds(k * rows, rows)
        total = lax.dot_general(
            cot_ref[k * rows : (k + 1) * rows, :],
            weight_ref[...],
            (((1,), (1,)), ((), ())),
            preferred_element_type=F32,
        )
        back_ref[k * rows : (k + 1) * rows, :] = (total * inverse).astype(BF16)
        stores.append(pltpu.make_async_copy(back_ref.at[span], back.at[span], sems.at[1 + k]))
        stores[-1].start()
    for store in stores:
        store.wait()


def pair_kernel(keep_ref, came_ref, *out_refs):
    chip = lax.axis_index("dp") // 2
    for offset, out_ref in enumerate(out_refs):
        there = jnp.bitwise_xor(chip, offset)
        total = keep_ref[there].astype(F32) + came_ref[there].astype(F32)
        out_ref[...] = total.astype(BF16)


def finish_kernel(
    share,
    own_ref,
    seed_ref,
    cross_ref,
    cycle_ref,
    last_ref,
    weight_ref,
    threshold_ref,
    *refs,
):
    vote_refs, (new_weight, keys, weight_out, keys_out, sems) = refs[:-5], refs[-5:]
    first = pl.multiple_of(lax.axis_index("dp") * share, share)
    votes = vote_refs[0][...].astype(F32)
    for ref in vote_refs[1:]:
        votes = votes + ref[...].astype(F32)
    limits = threshold_ref[:, pl.ds(first, share)].astype(F32)
    update = jnp.clip(votes / limits, -1.0, 1.0)
    old = weight_ref[:, pl.ds(first, share)].astype(F32)
    weight_out[...] = (old - 0.5 * update).astype(BF16)
    weight_copy = pltpu.make_async_copy(weight_out, new_weight, sems.at[0])
    weight_copy.start()

    outer = is_outer(lax.axis_index("tensor"))
    total = own_ref[...].astype(F32) + last_ref[...].astype(F32)

    @pl.when(outer)
    def _():
        keys_out[...] = (total + seed_ref[...].astype(F32)).astype(BF16)

    @pl.when(jnp.logical_not(outer))
    def _():
        more = cross_ref[...].astype(F32) + cycle_ref[...].astype(F32)
        keys_out[...] = (total + more).astype(BF16)

    keys_copy = pltpu.make_async_copy(keys_out, keys, sems.at[1])
    keys_copy.start()
    weight_copy.wait()
    keys_copy.wait()


def in_hbm(array):
    return pltpu.with_memory_space_constraint(array, pltpu.HBM)


def call(kernel, bound, outs, args, in_specs=None, out_specs=None, scratch=(), limit=VMEM_LIMIT):
    def body(*refs):
        kernel(*bound, *refs)

    return pl.pallas_call(
        body,
        out_shape=outs,
        in_specs=in_specs or [IN_VMEM] * len(args),
        out_specs=out_specs or [IN_VMEM] * len(outs),
        scratch_shapes=scratch,
        compiler_params=pltpu.CompilerParams(vmem_limit_bytes=limit),
    )(*args)


def on_line_of_four(tokens, cotangent, weight, momentum, threshold):
    depth, width = weight.shape
    n_dp, n_tensor = lax.axis_size("dp"), lax.axis_size("tensor")
    n_chips = n_dp // 2
    rows = tokens.shape[0] // n_tensor
    share = width // n_dp
    inverse = (depth * n_tensor) ** (-0.5)
    dma = pltpu.SemaphoreType.DMA

    def along(value, goal):
        pairs = []
        for d in range(n_dp):
            for plane in range(n_tensor):
                to = goal[plane]
                there = d * n_tensor + to if to is not None else (d ^ 1) * n_tensor + plane
                pairs.append((d * n_tensor + plane, there))
        return lax.ppermute(value, ("dp", "tensor"), pairs)

    def over(value, mask):
        return lax.ppermute(value, "dp", [(i, i ^ mask) for i in range(n_dp)])

    block = shaped(rows, width)
    seed, near, tokens, weight, cotangent = call(
        first_kernel,
        (inverse, rows),
        [block, block, shaped(*tokens.shape), shaped(*weight.shape), shaped(*cotangent.shape)],
        (in_hbm(tokens), in_hbm(weight), in_hbm(cotangent)),
        in_specs=[IN_HBM] * 3,
        scratch=[dma((5 + depth // TILE,))],
    )
    seed_came = along(seed, (1, 0, 3, 2))
    cross_came = along(near, (None, 2, 1, None))

    votes_shape = shaped(n_chips, depth, share)
    fresh, send, keep = call(
        momentum_kernel,
        (0.1 * inverse, share),
        [shaped(depth, width), votes_shape, votes_shape],
        (tokens, cotangent, momentum),
    )
    came = over(send, 1)

    third, own = call(rest_kernel, (inverse, rows), [block] * 2, (tokens, weight))
    cycle_came = along(third, (2, 0, 3, 1))

    sums = call(pair_kernel, (), [shaped(depth, share)] * n_chips, (keep, came))
    votes = [sums[0]] + [over(sums[k], 2 * k) for k in range(1, n_chips)]

    (relay,) = call(relay_kernel, (), [block], (third, near, seed_came))
    last_came = along(relay, (1, 3, 0, 2))

    input_grad, new_momentum = call(
        back_kernel,
        (inverse,),
        [shaped(*tokens.shape), shaped(1, depth, width)],
        (cotangent, weight, fresh),
        out_specs=[IN_HBM] * 2,
        scratch=[pltpu.VMEM(tokens.shape, BF16), dma((3,))],
    )
    new_weight, key_values = call(
        finish_kernel,
        (share,),
        [shaped(depth, share), block],
        (own, seed_came, cross_came, cycle_came, last_came, weight, threshold.reshape(1, width))
        + tuple(votes),
        out_specs=[IN_HBM] * 2,
        scratch=[pltpu.VMEM((depth, share), BF16), pltpu.VMEM((rows, width), BF16), dma((2,))],
    )
    return key_values, input_grad, new_momentum, new_weight


def in_general(tokens, cotangent, weight, momentum, threshold):
    inverse = (weight.shape[0] * lax.axis_size("tensor")) ** (-0.5)
    key_values = lax.psum_scatter(
        (jnp.dot(tokens, weight, preferred_element_type=F32) * inverse).astype(BF16),
        "tensor",
        scatter_dimension=0,
        tiled=True,
    )
    input_grad = (
        lax.dot_general(cotangent, weight, (((1,), (1,)), ((), ())), preferred_element_type=F32)
        * inverse
    ).astype(BF16)
    gradient = inverse * lax.dot_general(
        tokens, cotangent, (((0,), (0,)), ((), ())), preferred_element_type=F32
    )
    fresh = (0.9 * momentum[0].astype(F32) + 0.1 * gradient).astype(BF16)
    share = weight.shape[1] // lax.axis_size("dp")
    arrived = lax.all_to_all(fresh[None], "dp", split_axis=2, concat_axis=0, tiled=True)
    votes = jnp.sum(jnp.clip(arrived.astype(F32) / 0.125, -1.0, 1.0), axis=0)
    first = lax.axis_index("dp") * share
    own_columns = lax.dynamic_slice_in_dim(weight, first, share, 1)
    own_limits = lax.dynamic_slice_in_dim(threshold, first, share, 0)
    update = jnp.clip(votes / own_limits.astype(F32)[None, :], -1.0, 1.0)
    new_weight = (own_columns.astype(F32) - 0.5 * update).astype(BF16)
    return key_values, input_grad, fresh[None], new_weight


def solution(mesh):
    n_dp, n_tensor = mesh.shape["dp"], mesh.shape["tensor"]

    def per_device(tokens, cotangent, weight, momentum, threshold):
        depth, width = weight.shape
        fits = n_tensor == 4 and n_dp == 8 and width % (n_dp * LANES) == 0 and depth % TILE == 0
        chosen = on_line_of_four if fits else in_general
        return chosen(tokens, cotangent, weight, momentum, threshold)

    in_specs = (P("dp", "tensor"), P("dp", None), P("tensor", None), P("dp", "tensor", None), P())
    out_specs = (
        P(("dp", "tensor"), None),
        P("dp", "tensor"),
        P("dp", "tensor", None),
        P("tensor", "dp"),
    )
    return jax.shard_map(
        per_device, mesh=mesh, in_specs=in_specs, out_specs=out_specs, check_vma=False
    )
```

time: 78.4 us -> 29.6 us (0.38)
  other arithmetic: 20.5 us -> 0 us
  local copies, waits for them, and re-layouts: 15.1 us -> 0.27 us
  between operations: 14.1 us -> 0.7 us
  matrix products: 9.39 us -> 0 us
  Pallas kernels: 0 us -> 7.12 us
  starting transfers between devices: 5.41 us -> 11.5 us
  waiting for transfers between devices: 13.5 us -> 9.82 us
    all_to_all x1 -> x0, waiting for transfers between devices: 13.5 us -> none  [per_device(): lax.all_to_all(fresh[None], 'dp', split_axis=2, concat_axis=0, tiled=True)]
    ppermute x0 -> x8, starting transfers between devices: none -> 11.5 us  [the longest x4 7.4 us: along(): return lax.ppermute(value, ('dp', 'tensor'), pairs)]
    unnamed x1 -> x0, other arithmetic: 11.2 us -> none
    ppermute x0 -> x8, waiting for transfers between devices: none -> 9.82 us  [the longest x4 9.51 us: along(): return lax.ppermute(value, ('dp', 'tensor'), pairs)]
    dot_general x3 -> x0, matrix products: 9.39 us -> none  [the longest x1 3.16 us: per_device(): lax.dot_general(tokens, cotangent, (((0,), (0,)), ((), ())), preferred_el...]
    unnamed x10 -> x4, local copies, waits for them, and re-layouts: 9.15 us -> 0.27 us
    pallas_call x0 -> x7, Pallas kernels: none -> 7.12 us  [call(): pl.pallas_call(body, out_shape=outs, in_specs=in_specs or [IN_VMEM] * len...]
    min x1 -> x0, other arithmetic: 6.23 us -> none  [per_device(): jnp.clip(arrived.astype(jnp.float32) / 0.125, -1.0, 1.0)]
  transfers between devices with their start and end apart: 2 -> 8, of which waited for: 1 -> 3; matrix products, arithmetic and copies ran while one was open for 29% -> 0% of each run, Pallas kernels for 0% -> 9%
where the time goes in v3:
time: 29.6 us; the launch traced here: 29.4 us
  starting transfers between devices  11.5 us (39%)
  waiting for transfers between devices  9.82 us (33%)
  Pallas kernels  7.12 us (24%)
  between operations  0.7 us (2%)
    ppermute x4, waiting for transfers between devices, along(): return lax.ppermute(value, ('dp', 'tensor'), pairs)  9.51 us
    ppermute x4, starting transfers between devices, along(): return lax.ppermute(value, ('dp', 'tensor'), pairs)  7.4 us
    pallas_call x7, Pallas kernels, call(): pl.pallas_call(body, out_shape=outs, in_specs=in_specs or [IN_VMEM] * len...  7.12 us
    ppermute x4, starting transfers between devices, over(): return lax.ppermute(value, 'dp', [(i, i ^ mask) for i in range(n_dp)])  4.11 us
  transfers between devices with their start and end apart: 8, of which 3 were waited for; matrix products, arithmetic and copies ran while one was open for 0% of the time, Pallas kernels for 9%

profile of v3, /device:TPU:0, one launch (start us, length us, event | category | flops | bytes accessed | tf_op | source)
XLA Modules:
  0.0 29.4 jit_solution(8098627841775694440)
XLA Ops:
  0.6 0.0 copy-start
  0.6 2.2 %shard_map.84 = (bf16[128,1024]{1,0:T(8,128)(2,1)S(1)}, bf16[128,1024]{1,0:T(8,128)(2,1)S(1)}, bf16[512,768]{1,0:T(8,128)(2,1)S(1)}, bf16[768,1024]{1,0:T(8,128)(2,1)S(1)}, bf16[512,1024]{1,0:T(8,128)(2,1)S(1)}) custom-call(bf16[512,768]{1,0:T(8,128)(2,1)} %refs_0_.1, bf16[768,1024]{1,0:T(8,128)(2,1)} %refs_1_.1, bf16[512,1024]{1,0:T(8,128)(2,1)} %refs_2_.2), custom_call_target="tpu_custom_call" | custom-call | tf_op jit(solution)/shard_map/pallas_call | solution.py:202
  2.9 0.3 copy-done
  3.1 1.3 %shard_map.87 = (bf16[768,1024]{1,0:T(8,128)(2,1)S(1)}, bf16[4,768,128]{2,1,0:T(8,128)(2,1)S(1)}, bf16[4,768,128]{2,1,0:T(8,128)(2,1)S(1)}) custom-call(bf16[512,768]{1,0:T(8,128)(2,1)S(1)} %get-tuple-element.22.refs_0_, bf16[512,1024]{1,0:T(8,128)(2,1)S(1)} %get-tuple-element.28.refs_1_.refs_0_, bf16[1,768,1024]{2,1,0:T(8,128)(2,1)S(1)} %copy-done), custom_call_target="tpu_custom_call" | custom-call | tf_op jit(solution)/shard_map/pallas_call | solution.py:202
  4.4 0.6 %collective-permute-start.4 = (bf16[4,768,128]{2,1,0:T(8,128)(2,1)S(1)}, bf16[4,768,128]{2,1,0:T(8,128)(2,1)S(1)}, u32[]{:S(2)}, u32[]{:S(2)}) collective-permute-start(bf16[4,768,128]{2,1,0:T(8,128)(2,1)S(1)} %get-tuple-element.30), channel_id=1, source_target_pairs={{0,4},{4,0},{8,12},{12,8},{16,20},{20,16},{24,28},{28,24},{1,5},{5... | collective-permute-start | bytes 2359304 | tf_op jit(solution)/shard_map/ppermute | solution.py:231
  5.0 2.6 %collective-permute-start = (bf16[128,1024]{1,0:T(8,128)(2,1)S(1)}, bf16[128,1024]{1,0:T(8,128)(2,1)S(1)}, u32[]{:S(2)}, u32[]{:S(2)}) collective-permute-start(bf16[128,1024]{1,0:T(8,128)(2,1)S(1)} %get-tuple-element.25), channel_id=1, source_target_pairs={{0,1},{1,0},{2,3},{3,2},{4,5},{5,4},{6,7},{7,6},{8,9},{9,8},{10,11... | collective-permute-start | bytes 786440 | tf_op jit(solution)/shard_map/ppermute | solution.py:228
  7.6 0.2 collective-permute-start.1
  7.8 0.6 %shard_map.85 = (bf16[128,1024]{1,0:T(8,128)(2,1)S(1)}, bf16[128,1024]{1,0:T(8,128)(2,1)S(1)}) custom-call(bf16[512,768]{1,0:T(8,128)(2,1)S(1)} %get-tuple-element.22.refs_0_, bf16[768,1024]{1,0:T(8,128)(2,1)S(1)} %get-tuple-element.23.refs_1_.refs_5_), custom_call_target="tpu_custom_call" | custom-call | tf_op jit(solution)/shard_map/pallas_call | solution.py:202
  8.4 2.5 %collective-permute-start.2 = (bf16[128,1024]{1,0:T(8,128)(2,1)S(1)}, bf16[128,1024]{1,0:T(8,128)(2,1)S(1)}, u32[]{:S(2)}, u32[]{:S(2)}) collective-permute-start(bf16[128,1024]{1,0:T(8,128)(2,1)S(1)} %get-tuple-element.27.refs_0_), channel_id=1, source_target_pairs={{0,2},{1,0},{2,3},{3,1},{4,6},{5,4},{6,7},{7,5},{8,10},{9,8},{10,1... | collective-permute-start | bytes 786440 | tf_op jit(solution)/shard_map/ppermute | solution.py:228
  10.9 3.9 %collective-permute-done.refs_2_.refs_1_ = bf16[128,1024]{1,0:T(8,128)(2,1)S(1)} collective-permute-done((bf16[128,1024]{1,0:T(8,128)(2,1)S(1)}, bf16[128,1024]{1,0:T(8,128)(2,1)S(1)}, u32[]{:S(2)}, u32[]{:S(2)}) %collective-permute-start) | collective-permute-done | bytes 262176 | tf_op jit(solution)/shard_map/ppermute | solution.py:228
  14.8 2.1 %collective-permute-start.3 = (bf16[128,1024]{1,0:T(8,128)(2,1)S(1)}, bf16[128,1024]{1,0:T(8,128)(2,1)S(1)}, u32[]{:S(2)}, u32[]{:S(2)}) collective-permute-start(bf16[128,1024]{1,0:T(8,128)(2,1)S(1)} %shard_map.86), channel_id=1, source_target_pairs={{0,1},{1,3},{2,0},{3,2},{4,5},{5,7},{6,4},{7,6},{8,9},{9,11},{10,8... | collective-permute-start | bytes 786440 | tf_op jit(solution)/shard_map/ppermute | solution.py:228
  16.9 0.0 collective-permute-done.4.refs_1_
  16.9 0.2 shard_map.88
  17.1 1.6 %collective-permute-start.5 = (bf16[768,128]{1,0:T(8,128)(2,1)S(1)}, bf16[768,128]{1,0:T(8,128)(2,1)S(1)}, u32[]{:S(2)}, u32[]{:S(2)}) collective-permute-start(bf16[768,128]{1,0:T(8,128)(2,1)S(1)} %get-tuple-element.32), channel_id=1, source_target_pairs={{0,8},{4,12},{8,0},{12,4},{16,24},{20,28},{24,16},{28,20},{1,9},{5... | collective-permute-start | bytes 589832 | tf_op jit(solution)/shard_map/ppermute | solution.py:231
  18.7 1.5 %collective-permute-start.6 = (bf16[768,128]{1,0:T(8,128)(2,1)S(1)}, bf16[768,128]{1,0:T(8,128)(2,1)S(1)}, u32[]{:S(2)}, u32[]{:S(2)}) collective-permute-start(bf16[768,128]{1,0:T(8,128)(2,1)S(1)} %get-tuple-element.33), channel_id=1, source_target_pairs={{0,16},{4,20},{8,24},{12,28},{16,0},{20,4},{24,8},{28,12},{1,17},{... | collective-permute-start | bytes 589832 | tf_op jit(solution)/shard_map/ppermute | solution.py:231
  20.2 0.0 collective-permute-done.1.refs_2_
  20.2 0.5 %collective-permute-start.7 = (bf16[768,128]{1,0:T(8,128)(2,1)S(1)}, bf16[768,128]{1,0:T(8,128)(2,1)S(1)}, u32[]{:S(2)}, u32[]{:S(2)}) collective-permute-start(bf16[768,128]{1,0:T(8,128)(2,1)S(1)} %get-tuple-element.34), channel_id=1, source_target_pairs={{0,24},{4,28},{8,16},{12,20},{16,8},{20,12},{24,0},{28,4},{1,25},{... | collective-permute-start | bytes 589832 | tf_op jit(solution)/shard_map/ppermute | solution.py:231
  20.7 0.0 copy-start.1
  20.7 1.8 %shard_map.90 = (bf16[512,768]{1,0:T(8,128)(2,1)}, bf16[1,768,1024]{2,1,0:T(8,128)(2,1)}) custom-call(bf16[512,1024]{1,0:T(8,128)(2,1)S(1)} %get-tuple-element.28.refs_1_.refs_0_, bf16[768,1024]{1,0:T(8,128)(2,1)S(1)} %get-tuple-element.23.refs_1_.refs_5_, bf16[768,1024]{1,0:T(8,128)(2,1)S(1)} %get-tuple-element.36.refs_2_), custom_call_target="tpu_custom_call" | custom-call | tf_op jit(solution)/shard_map/pallas_call | solution.py:202
  22.5 0.0 collective-permute-done.2.refs_3_
  22.5 5.6 %collective-permute-done.3.refs_4_ = bf16[128,1024]{1,0:T(8,128)(2,1)S(1)} collective-permute-done((bf16[128,1024]{1,0:T(8,128)(2,1)S(1)}, bf16[128,1024]{1,0:T(8,128)(2,1)S(1)}, u32[]{:S(2)}, u32[]{:S(2)}) %collective-permute-start.3) | collective-permute-done | bytes 262176 | tf_op jit(solution)/shard_map/ppermute | solution.py:228
  28.1 0.0 collective-permute-done.5.refs_8_
  28.1 0.3 %collective-permute-done.6.refs_9_ = bf16[768,128]{1,0:T(8,128)(2,1)S(1)} collective-permute-done((bf16[768,128]{1,0:T(8,128)(2,1)S(1)}, bf16[768,128]{1,0:T(8,128)(2,1)S(1)}, u32[]{:S(2)}, u32[]{:S(2)}) %collective-permute-start.6) | collective-permute-done | bytes 196640 | tf_op jit(solution)/shard_map/ppermute | solution.py:231
  28.4 0.0 collective-permute-done.7.refs_10_
  28.4 0.0 copy-done.1
  28.4 1.0 %shard_map.89 = (bf16[768,128]{1,0:T(8,128)(2,1)}, bf16[128,1024]{1,0:T(8,128)(2,1)}) custom-call(bf16[128,1024]{1,0:T(8,128)(2,1)S(1)} %get-tuple-element.24.refs_0_, bf16[128,1024]{1,0:T(8,128)(2,1)S(1)} %collective-permute-done.refs_2_.refs_1_, bf16[128,1024]{1,0:T(8,128)(2,1)S(1)} %collective-permute-done.1.refs_2_, ...), custom_call_target="tpu_custom_call" | custom-call | tf_op jit(solution)/shard_map/pallas_call | solution.py:202
  (1 shorter events, 0.0 us)
Async XLA Ops:
  0.6 2.5 %copy-start = (bf16[1,768,1024]{2,1,0:T(8,128)(2,1)S(1)}, bf16[1,768,1024]{2,1,0:T(8,128)(2,1)}, u32[]{:S(2)}) copy-start(bf16[1,768,1024]{2,1,0:T(8,128)(2,1)} %refs_2_.3) | copy-start | bytes 4718596
  4.4 12.5 %collective-permute-start.4 = (bf16[4,768,128]{2,1,0:T(8,128)(2,1)S(1)}, bf16[4,768,128]{2,1,0:T(8,128)(2,1)S(1)}, u32[]{:S(2)}, u32[]{:S(2)}) collective-permute-start(bf16[4,768,128]{2,1,0:T(8,128)(2,1)S(1)} %get-tuple-element.30), channel_id=1, source_target_pairs={{0,4},{4,0},{8,12},{12,8},{16,20},{20,16},{24,28},{28,24},{1,5},{5... | collective-permute-start | bytes 2359304 | tf_op jit(solution)/shard_map/ppermute | solution.py:231
  5.0 9.8 %collective-permute-start = (bf16[128,1024]{1,0:T(8,128)(2,1)S(1)}, bf16[128,1024]{1,0:T(8,128)(2,1)S(1)}, u32[]{:S(2)}, u32[]{:S(2)}) collective-permute-start(bf16[128,1024]{1,0:T(8,128)(2,1)S(1)} %get-tuple-element.25), channel_id=1, source_target_pairs={{0,1},{1,0},{2,3},{3,2},{4,5},{5,4},{6,7},{7,6},{8,9},{9,8},{10,11... | collective-permute-start | bytes 786440 | tf_op jit(solution)/shard_map/ppermute | solution.py:228
  7.6 12.6 %collective-permute-start.1 = (bf16[128,1024]{1,0:T(8,128)(2,1)S(1)}, bf16[128,1024]{1,0:T(8,128)(2,1)S(1)}, u32[]{:S(2)}, u32[]{:S(2)}) collective-permute-start(bf16[128,1024]{1,0:T(8,128)(2,1)S(1)} %get-tuple-element.26.refs_1_), channel_id=1, source_target_pairs={{0,4},{1,2},{2,1},{3,7},{4,0},{5,6},{6,5},{7,3},{8,12},{9,10},{10,... | collective-permute-start | bytes 786440 | tf_op jit(solution)/shard_map/ppermute | solution.py:228
  8.4 14.1 %collective-permute-start.2 = (bf16[128,1024]{1,0:T(8,128)(2,1)S(1)}, bf16[128,1024]{1,0:T(8,128)(2,1)S(1)}, u32[]{:S(2)}, u32[]{:S(2)}) collective-permute-start(bf16[128,1024]{1,0:T(8,128)(2,1)S(1)} %get-tuple-element.27.refs_0_), channel_id=1, source_target_pairs={{0,2},{1,0},{2,3},{3,1},{4,6},{5,4},{6,7},{7,5},{8,10},{9,8},{10,1... | collective-permute-start | bytes 786440 | tf_op jit(solution)/shard_map/ppermute | solution.py:228
  14.8 13.3 %collective-permute-start.3 = (bf16[128,1024]{1,0:T(8,128)(2,1)S(1)}, bf16[128,1024]{1,0:T(8,128)(2,1)S(1)}, u32[]{:S(2)}, u32[]{:S(2)}) collective-permute-start(bf16[128,1024]{1,0:T(8,128)(2,1)S(1)} %shard_map.86), channel_id=1, source_target_pairs={{0,1},{1,3},{2,0},{3,2},{4,5},{5,7},{6,4},{7,6},{8,9},{9,11},{10,8... | collective-permute-start | bytes 786440 | tf_op jit(solution)/shard_map/ppermute | solution.py:228
  17.1 11.0 %collective-permute-start.5 = (bf16[768,128]{1,0:T(8,128)(2,1)S(1)}, bf16[768,128]{1,0:T(8,128)(2,1)S(1)}, u32[]{:S(2)}, u32[]{:S(2)}) collective-permute-start(bf16[768,128]{1,0:T(8,128)(2,1)S(1)} %get-tuple-element.32), channel_id=1, source_target_pairs={{0,8},{4,12},{8,0},{12,4},{16,24},{20,28},{24,16},{28,20},{1,9},{5... | collective-permute-start | bytes 589832 | tf_op jit(solution)/shard_map/ppermute | solution.py:231
  18.7 9.7 %collective-permute-start.6 = (bf16[768,128]{1,0:T(8,128)(2,1)S(1)}, bf16[768,128]{1,0:T(8,128)(2,1)S(1)}, u32[]{:S(2)}, u32[]{:S(2)}) collective-permute-start(bf16[768,128]{1,0:T(8,128)(2,1)S(1)} %get-tuple-element.33), channel_id=1, source_target_pairs={{0,16},{4,20},{8,24},{12,28},{16,0},{20,4},{24,8},{28,12},{1,17},{... | collective-permute-start | bytes 589832 | tf_op jit(solution)/shard_map/ppermute | solution.py:231
  20.2 8.2 %collective-permute-start.7 = (bf16[768,128]{1,0:T(8,128)(2,1)S(1)}, bf16[768,128]{1,0:T(8,128)(2,1)S(1)}, u32[]{:S(2)}, u32[]{:S(2)}) collective-permute-start(bf16[768,128]{1,0:T(8,128)(2,1)S(1)} %get-tuple-element.34), channel_id=1, source_target_pairs={{0,24},{4,28},{8,16},{12,20},{16,8},{20,12},{24,0},{28,4},{1,25},{... | collective-permute-start | bytes 589832 | tf_op jit(solution)/shard_map/ppermute | solution.py:231
  20.7 7.7 %copy-start.1 = (s32[1024]{0:T(1024)S(1)}, s32[1024]{0:T(1024)}, u32[]{:S(2)}) copy-start(s32[1024]{0:T(1024)} %param.9) | copy-start | bytes 12292

commit v4 on v3

--- a/solution.py
+++ b/solution.py
@@ -143,25 +143,19 @@
 
 
 def pair_kernel(keep_ref, came_ref, *out_refs):
-    chip = lax.axis_index("dp") // 2
-    for offset, out_ref in enumerate(out_refs):
-        there = jnp.bitwise_xor(chip, offset)
+    place = lax.axis_index("dp")
+    for step, out_ref in enumerate(out_refs):
+        there = jnp.bitwise_xor(place // 2, chip_offset(place, step))
         total = keep_ref[there].astype(F32) + came_ref[there].astype(F32)
         out_ref[...] = total.astype(BF16)
 
 
-def finish_kernel(
-    share,
-    own_ref,
-    seed_ref,
-    cross_ref,
-    cycle_ref,
-    last_ref,
-    weight_ref,
-    threshold_ref,
-    *refs,
-):
-    vote_refs, (new_weight, keys, weight_out, keys_out, sems) = refs[:-5], refs[-5:]
+def chip_offset(place, step):
+    return step if step in (0, 3) else 1 + (step - 1 + place) % 2
+
+
+def update_kernel(share, weight_ref, threshold_ref, *refs):
+    vote_refs, out_ref = refs[:-1], refs[-1]
     first = pl.multiple_of(lax.axis_index("dp") * share, share)
     votes = vote_refs[0][...].astype(F32)
     for ref in vote_refs[1:]:
@@ -169,23 +163,36 @@
     limits = threshold_ref[:, pl.ds(first, share)].astype(F32)
     update = jnp.clip(votes / limits, -1.0, 1.0)
     old = weight_ref[:, pl.ds(first, share)].astype(F32)
-    weight_out[...] = (old - 0.5 * update).astype(BF16)
-    weight_copy = pltpu.make_async_copy(weight_out, new_weight, sems.at[0])
+    out_ref[...] = (old - 0.5 * update).astype(BF16)
+
+
+def keys_kernel(
+    own_ref,
+    seed_ref,
+    cross_ref,
+    cycle_ref,
+    last_ref,
+    updated_ref,
+    keys,
+    new_weight,
+    keys_ref,
+    sems,
+):
+    weight_copy = pltpu.make_async_copy(updated_ref, new_weight, sems.at[0])
     weight_copy.start()
-
     outer = is_outer(lax.axis_index("tensor"))
     total = own_ref[...].astype(F32) + last_ref[...].astype(F32)
 
     @pl.when(outer)
     def _():
-        keys_out[...] = (total + seed_ref[...].astype(F32)).astype(BF16)
+        keys_ref[...] = (total + seed_ref[...].astype(F32)).astype(BF16)
 
     @pl.when(jnp.logical_not(outer))
     def _():
         more = cross_ref[...].astype(F32) + cycle_ref[...].astype(F32)
-        keys_out[...] = (total + more).astype(BF16)
-
-    keys_copy = pltpu.make_async_copy(keys_out, keys, sems.at[1])
+        keys_ref[...] = (total + more).astype(BF16)
+
+    keys_copy = pltpu.make_async_copy(keys_ref, keys, sems.at[1])
     keys_copy.start()
     weight_copy.wait()
     keys_copy.wait()
@@ -227,8 +234,8 @@
                 pairs.append((d * n_tensor + plane, there))
         return lax.ppermute(value, ("dp", "tensor"), pairs)
 
-    def over(value, mask):
-        return lax.ppermute(value, "dp", [(i, i ^ mask) for i in range(n_dp)])
+    def over(value, goal):
+        return lax.ppermute(value, "dp", [(i, goal(i)) for i in range(n_dp)])
 
     block = shaped(rows, width)
     seed, near, tokens, weight, cotangent = call(
@@ -249,13 +256,16 @@
         [shaped(depth, width), votes_shape, votes_shape],
         (tokens, cotangent, momentum),
     )
-    came = over(send, 1)
+    came = over(send, lambda i: i ^ 1)
 
     third, own = call(rest_kernel, (inverse, rows), [block] * 2, (tokens, weight))
     cycle_came = along(third, (2, 0, 3, 1))
 
     sums = call(pair_kernel, (), [shaped(depth, share)] * n_chips, (keep, came))
-    votes = [sums[0]] + [over(sums[k], 2 * k) for k in range(1, n_chips)]
+    votes = [sums[0]] + [
+        over(sums[k], lambda i, k=k: i ^ (2 * chip_offset(i, k)))
+        for k in range(1, n_chips)
+    ]
 
     (relay,) = call(relay_kernel, (), [block], (third, near, seed_came))
     last_came = along(relay, (1, 3, 0, 2))
@@ -268,14 +278,19 @@
         out_specs=[IN_HBM] * 2,
         scratch=[pltpu.VMEM(tokens.shape, BF16), dma((3,))],
     )
-    new_weight, key_values = call(
-        finish_kernel,
+    (updated,) = call(
+        update_kernel,
         (share,),
-        [shaped(depth, share), block],
-        (own, seed_came, cross_came, cycle_came, last_came, weight, threshold.reshape(1, width))
-        + tuple(votes),
+        [shaped(depth, share)],
+        (weight, threshold.reshape(1, width)) + tuple(votes),
+    )
+    key_values, new_weight = call(
+        keys_kernel,
+        (),
+        [block, shaped(depth, share)],
+        (own, seed_came, cross_came, cycle_came, last_came, updated),
         out_specs=[IN_HBM] * 2,
-        scratch=[pltpu.VMEM((depth, share), BF16), pltpu.VMEM((rows, width), BF16), dma((2,))],
+        scratch=[pltpu.VMEM((rows, width), BF16), dma((2,))],
     )
     return key_values, input_grad, new_momentum, new_weight
 

time: 29.6 us -> 31.4 us (1.061)
  starting transfers between devices: 11.5 us -> 13.4 us
    ppermute x4, waiting for transfers between devices: 9.51 us -> 4.6 us  [along(): return lax.ppermute(value, ('dp', 'tensor'), pairs)]
    ppermute x4, waiting for transfers between devices: 0.31 us -> 5.12 us  [over(): return lax.ppermute(value, 'dp', [(i, goal(i)) for i in range(n_dp)])]
    ppermute x4, starting transfers between devices: 4.11 us -> 5.71 us  [over(): return lax.ppermute(value, 'dp', [(i, goal(i)) for i in range(n_dp)])]
    pallas_call x7 -> x8, Pallas kernels: 7.12 us -> 7.14 us  [call(): pl.pallas_call(body, out_shape=outs, in_specs=in_specs or [IN_VMEM] * len...]
where the time goes in v4:
time: 31.4 us; the launch traced here: 31.2 us
  starting transfers between devices  13.4 us (43%)
  waiting for transfers between devices  9.71 us (31%)
  Pallas kernels  7.14 us (23%)
  between operations  0.71 us (2%)
    ppermute x4, starting transfers between devices, along(): return lax.ppermute(value, ('dp', 'tensor'), pairs)  7.68 us
    pallas_call x8, Pallas kernels, call(): pl.pallas_call(body, out_shape=outs, in_specs=in_specs or [IN_VMEM] * len...  7.14 us
    ppermute x4, starting transfers between devices, over(): return lax.ppermute(value, 'dp', [(i, goal(i)) for i in range(n_dp)])  5.71 us
    ppermute x4, waiting for transfers between devices, over(): return lax.ppermute(value, 'dp', [(i, goal(i)) for i in range(n_dp)])  5.12 us
    ppermute x4, waiting for transfers between devices, along(): return lax.ppermute(value, ('dp', 'tensor'), pairs)  4.6 us
  transfers between devices with their start and end apart: 8, of which 3 were waited for; matrix products, arithmetic and copies ran while one was open for 0% of the time, Pallas kernels for 9%

profile of v4, /device:TPU:0, one launch (start us, length us, event | category | flops | bytes accessed | tf_op | source)
XLA Modules:
  0.0 31.2 jit_solution(12373209880001346210)
XLA Ops:
  0.6 0.0 copy-start
  0.6 2.2 %shard_map.84 = (bf16[128,1024]{1,0:T(8,128)(2,1)S(1)}, bf16[128,1024]{1,0:T(8,128)(2,1)S(1)}, bf16[512,768]{1,0:T(8,128)(2,1)S(1)}, bf16[768,1024]{1,0:T(8,128)(2,1)S(1)}, bf16[512,1024]{1,0:T(8,128)(2,1)S(1)}) custom-call(bf16[512,768]{1,0:T(8,128)(2,1)} %refs_0_.1, bf16[768,1024]{1,0:T(8,128)(2,1)} %refs_1_.1, bf16[512,1024]{1,0:T(8,128)(2,1)} %refs_2_.2), custom_call_target="tpu_custom_call" | custom-call | tf_op jit(solution)/shard_map/pallas_call | solution.py:209
  2.9 0.3 copy-done
  3.1 1.3 %shard_map.87 = (bf16[768,1024]{1,0:T(8,128)(2,1)S(1)}, bf16[4,768,128]{2,1,0:T(8,128)(2,1)S(1)}, bf16[4,768,128]{2,1,0:T(8,128)(2,1)S(1)}) custom-call(bf16[512,768]{1,0:T(8,128)(2,1)S(1)} %get-tuple-element.22.refs_0_, bf16[512,1024]{1,0:T(8,128)(2,1)S(1)} %get-tuple-element.28.refs_1_.refs_0_, bf16[1,768,1024]{2,1,0:T(8,128)(2,1)S(1)} %copy-done), custom_call_target="tpu_custom_call" | custom-call | tf_op jit(solution)/shard_map/pallas_call | solution.py:209
  4.4 0.6 %collective-permute-start.4 = (bf16[4,768,128]{2,1,0:T(8,128)(2,1)S(1)}, bf16[4,768,128]{2,1,0:T(8,128)(2,1)S(1)}, u32[]{:S(2)}, u32[]{:S(2)}) collective-permute-start(bf16[4,768,128]{2,1,0:T(8,128)(2,1)S(1)} %get-tuple-element.30), channel_id=1, source_target_pairs={{0,4},{4,0},{8,12},{12,8},{16,20},{20,16},{24,28},{28,24},{1,5},{5... | collective-permute-start | bytes 2359304 | tf_op jit(solution)/shard_map/ppermute | solution.py:238
  5.0 2.6 %collective-permute-start = (bf16[128,1024]{1,0:T(8,128)(2,1)S(1)}, bf16[128,1024]{1,0:T(8,128)(2,1)S(1)}, u32[]{:S(2)}, u32[]{:S(2)}) collective-permute-start(bf16[128,1024]{1,0:T(8,128)(2,1)S(1)} %get-tuple-element.25), channel_id=1, source_target_pairs={{0,1},{1,0},{2,3},{3,2},{4,5},{5,4},{6,7},{7,6},{8,9},{9,8},{10,11... | collective-permute-start | bytes 786440 | tf_op jit(solution)/shard_map/ppermute | solution.py:235
  7.6 0.0 collective-permute-done.4.refs_1_
  7.6 0.2 shard_map.88
  7.8 2.2 %collective-permute-start.5 = (bf16[768,128]{1,0:T(8,128)(2,1)S(1)}, bf16[768,128]{1,0:T(8,128)(2,1)S(1)}, u32[]{:S(2)}, u32[]{:S(2)}) collective-permute-start(bf16[768,128]{1,0:T(8,128)(2,1)S(1)} %get-tuple-element.32), channel_id=1, source_target_pairs={{0,8},{4,20},{8,0},{12,28},{16,24},{20,4},{24,16},{28,12},{1,9},{5... | collective-permute-start | bytes 589832 | tf_op jit(solution)/shard_map/ppermute | solution.py:238
  10.0 0.0 collective-permute-start.1
  10.0 0.6 %shard_map.85 = (bf16[128,1024]{1,0:T(8,128)(2,1)S(1)}, bf16[128,1024]{1,0:T(8,128)(2,1)S(1)}) custom-call(bf16[512,768]{1,0:T(8,128)(2,1)S(1)} %get-tuple-element.22.refs_0_, bf16[768,1024]{1,0:T(8,128)(2,1)S(1)} %get-tuple-element.23.refs_1_.refs_0_), custom_call_target="tpu_custom_call" | custom-call | tf_op jit(solution)/shard_map/pallas_call | solution.py:209
  10.6 3.1 %collective-permute-start.2 = (bf16[128,1024]{1,0:T(8,128)(2,1)S(1)}, bf16[128,1024]{1,0:T(8,128)(2,1)S(1)}, u32[]{:S(2)}, u32[]{:S(2)}) collective-permute-start(bf16[128,1024]{1,0:T(8,128)(2,1)S(1)} %get-tuple-element.27.refs_0_), channel_id=1, source_target_pairs={{0,2},{1,0},{2,3},{3,1},{4,6},{5,4},{6,7},{7,5},{8,10},{9,8},{10,1... | collective-permute-start | bytes 786440 | tf_op jit(solution)/shard_map/ppermute | solution.py:235
  13.7 1.1 %collective-permute-done.refs_2_.refs_1_ = bf16[128,1024]{1,0:T(8,128)(2,1)S(1)} collective-permute-done((bf16[128,1024]{1,0:T(8,128)(2,1)S(1)}, bf16[128,1024]{1,0:T(8,128)(2,1)S(1)}, u32[]{:S(2)}, u32[]{:S(2)}) %collective-permute-start) | collective-permute-done | bytes 262176 | tf_op jit(solution)/shard_map/ppermute | solution.py:235
  14.8 2.0 %collective-permute-start.3 = (bf16[128,1024]{1,0:T(8,128)(2,1)S(1)}, bf16[128,1024]{1,0:T(8,128)(2,1)S(1)}, u32[]{:S(2)}, u32[]{:S(2)}) collective-permute-start(bf16[128,1024]{1,0:T(8,128)(2,1)S(1)} %shard_map.86), channel_id=1, source_target_pairs={{0,1},{1,3},{2,0},{3,2},{4,5},{5,7},{6,4},{7,6},{8,9},{9,11},{10,8... | collective-permute-start | bytes 786440 | tf_op jit(solution)/shard_map/ppermute | solution.py:235
  16.8 1.7 %collective-permute-start.6 = (bf16[768,128]{1,0:T(8,128)(2,1)S(1)}, bf16[768,128]{1,0:T(8,128)(2,1)S(1)}, u32[]{:S(2)}, u32[]{:S(2)}) collective-permute-start(bf16[768,128]{1,0:T(8,128)(2,1)S(1)} %get-tuple-element.33), channel_id=1, source_target_pairs={{0,16},{4,12},{8,24},{12,4},{16,0},{20,28},{24,8},{28,20},{1,17},{... | collective-permute-start | bytes 589832 | tf_op jit(solution)/shard_map/ppermute | solution.py:238
  18.5 0.0 collective-permute-done.5.refs_3_
  18.5 1.3 %collective-permute-start.7 = (bf16[768,128]{1,0:T(8,128)(2,1)S(1)}, bf16[768,128]{1,0:T(8,128)(2,1)S(1)}, u32[]{:S(2)}, u32[]{:S(2)}) collective-permute-start(bf16[768,128]{1,0:T(8,128)(2,1)S(1)} %get-tuple-element.34), channel_id=1, source_target_pairs={{0,24},{4,28},{8,16},{12,20},{16,8},{20,12},{24,0},{28,4},{1,25},{... | collective-permute-start | bytes 589832 | tf_op jit(solution)/shard_map/ppermute | solution.py:238
  19.8 0.0 copy-start.1
  19.8 1.8 %shard_map.91 = (bf16[512,768]{1,0:T(8,128)(2,1)}, bf16[1,768,1024]{2,1,0:T(8,128)(2,1)}) custom-call(bf16[512,1024]{1,0:T(8,128)(2,1)S(1)} %get-tuple-element.28.refs_1_.refs_0_, bf16[768,1024]{1,0:T(8,128)(2,1)S(1)} %get-tuple-element.23.refs_1_.refs_0_, bf16[768,1024]{1,0:T(8,128)(2,1)S(1)} %get-tuple-element.36.refs_2_), custom_call_target="tpu_custom_call" | custom-call | tf_op jit(solution)/shard_map/pallas_call | solution.py:209
  21.6 5.1 %collective-permute-done.6.refs_4_ = bf16[768,128]{1,0:T(8,128)(2,1)S(1)} collective-permute-done((bf16[768,128]{1,0:T(8,128)(2,1)S(1)}, bf16[768,128]{1,0:T(8,128)(2,1)S(1)}, u32[]{:S(2)}, u32[]{:S(2)}) %collective-permute-start.6) | collective-permute-done | bytes 196640 | tf_op jit(solution)/shard_map/ppermute | solution.py:238
  26.7 0.0 collective-permute-done.7.refs_5_
  26.7 0.0 copy-done.1
  26.7 0.2 shard_map.89.refs_5_
  26.8 0.0 collective-permute-done.1.refs_2_
  26.9 0.0 collective-permute-done.2.refs_3_
  26.9 3.5 %collective-permute-done.3.refs_4_ = bf16[128,1024]{1,0:T(8,128)(2,1)S(1)} collective-permute-done((bf16[128,1024]{1,0:T(8,128)(2,1)S(1)}, bf16[128,1024]{1,0:T(8,128)(2,1)S(1)}, u32[]{:S(2)}, u32[]{:S(2)}) %collective-permute-start.3) | collective-permute-done | bytes 262176 | tf_op jit(solution)/shard_map/ppermute | solution.py:235
  30.4 0.9 %shard_map.90 = (bf16[128,1024]{1,0:T(8,128)(2,1)}, bf16[768,128]{1,0:T(8,128)(2,1)}) custom-call(bf16[128,1024]{1,0:T(8,128)(2,1)S(1)} %get-tuple-element.24.refs_0_, bf16[128,1024]{1,0:T(8,128)(2,1)S(1)} %collective-permute-done.refs_2_.refs_1_, bf16[128,1024]{1,0:T(8,128)(2,1)S(1)} %collective-permute-done.1.refs_2_, ...), custom_call_target="tpu_custom_call" | custom-call | tf_op jit(solution)/shard_map/pallas_call | solution.py:209
  (1 shorter events, 0.0 us)
Async XLA Ops:
  0.6 2.5 %copy-start = (bf16[1,768,1024]{2,1,0:T(8,128)(2,1)S(1)}, bf16[1,768,1024]{2,1,0:T(8,128)(2,1)}, u32[]{:S(2)}) copy-start(bf16[1,768,1024]{2,1,0:T(8,128)(2,1)} %refs_2_.3) | copy-start | bytes 4718596
  4.4 3.2 %collective-permute-start.4 = (bf16[4,768,128]{2,1,0:T(8,128)(2,1)S(1)}, bf16[4,768,128]{2,1,0:T(8,128)(2,1)S(1)}, u32[]{:S(2)}, u32[]{:S(2)}) collective-permute-start(bf16[4,768,128]{2,1,0:T(8,128)(2,1)S(1)} %get-tuple-element.30), channel_id=1, source_target_pairs={{0,4},{4,0},{8,12},{12,8},{16,20},{20,16},{24,28},{28,24},{1,5},{5... | collective-permute-start | bytes 2359304 | tf_op jit(solution)/shard_map/ppermute | solution.py:238
  5.0 9.8 %collective-permute-start = (bf16[128,1024]{1,0:T(8,128)(2,1)S(1)}, bf16[128,1024]{1,0:T(8,128)(2,1)S(1)}, u32[]{:S(2)}, u32[]{:S(2)}) collective-permute-start(bf16[128,1024]{1,0:T(8,128)(2,1)S(1)} %get-tuple-element.25), channel_id=1, source_target_pairs={{0,1},{1,0},{2,3},{3,2},{4,5},{5,4},{6,7},{7,6},{8,9},{9,8},{10,11... | collective-permute-start | bytes 786440 | tf_op jit(solution)/shard_map/ppermute | solution.py:235
  7.8 10.6 %collective-permute-start.5 = (bf16[768,128]{1,0:T(8,128)(2,1)S(1)}, bf16[768,128]{1,0:T(8,128)(2,1)S(1)}, u32[]{:S(2)}, u32[]{:S(2)}) collective-permute-start(bf16[768,128]{1,0:T(8,128)(2,1)S(1)} %get-tuple-element.32), channel_id=1, source_target_pairs={{0,8},{4,20},{8,0},{12,28},{16,24},{20,4},{24,16},{28,12},{1,9},{5... | collective-permute-start | bytes 589832 | tf_op jit(solution)/shard_map/ppermute | solution.py:238
  10.0 16.8 %collective-permute-start.1 = (bf16[128,1024]{1,0:T(8,128)(2,1)S(1)}, bf16[128,1024]{1,0:T(8,128)(2,1)S(1)}, u32[]{:S(2)}, u32[]{:S(2)}) collective-permute-start(bf16[128,1024]{1,0:T(8,128)(2,1)S(1)} %get-tuple-element.26.refs_1_), channel_id=1, source_target_pairs={{0,4},{1,2},{2,1},{3,7},{4,0},{5,6},{6,5},{7,3},{8,12},{9,10},{10,... | collective-permute-start | bytes 786440 | tf_op jit(solution)/shard_map/ppermute | solution.py:235
  10.6 16.2 %collective-permute-start.2 = (bf16[128,1024]{1,0:T(8,128)(2,1)S(1)}, bf16[128,1024]{1,0:T(8,128)(2,1)S(1)}, u32[]{:S(2)}, u32[]{:S(2)}) collective-permute-start(bf16[128,1024]{1,0:T(8,128)(2,1)S(1)} %get-tuple-element.27.refs_0_), channel_id=1, source_target_pairs={{0,2},{1,0},{2,3},{3,1},{4,6},{5,4},{6,7},{7,5},{8,10},{9,8},{10,1... | collective-permute-start | bytes 786440 | tf_op jit(solution)/shard_map/ppermute | solution.py:235
  14.8 15.5 %collective-permute-start.3 = (bf16[128,1024]{1,0:T(8,128)(2,1)S(1)}, bf16[128,1024]{1,0:T(8,128)(2,1)S(1)}, u32[]{:S(2)}, u32[]{:S(2)}) collective-permute-start(bf16[128,1024]{1,0:T(8,128)(2,1)S(1)} %shard_map.86), channel_id=1, source_target_pairs={{0,1},{1,3},{2,0},{3,2},{4,5},{5,7},{6,4},{7,6},{8,9},{9,11},{10,8... | collective-permute-start | bytes 786440 | tf_op jit(solution)/shard_map/ppermute | solution.py:235
  16.8 9.9 %collective-permute-start.6 = (bf16[768,128]{1,0:T(8,128)(2,1)S(1)}, bf16[768,128]{1,0:T(8,128)(2,1)S(1)}, u32[]{:S(2)}, u32[]{:S(2)}) collective-permute-start(bf16[768,128]{1,0:T(8,128)(2,1)S(1)} %get-tuple-element.33), channel_id=1, source_target_pairs={{0,16},{4,12},{8,24},{12,4},{16,0},{20,28},{24,8},{28,20},{1,17},{... | collective-permute-start | bytes 589832 | tf_op jit(solution)/shard_map/ppermute | solution.py:238
  18.5 8.2 %collective-permute-start.7 = (bf16[768,128]{1,0:T(8,128)(2,1)S(1)}, bf16[768,128]{1,0:T(8,128)(2,1)S(1)}, u32[]{:S(2)}, u32[]{:S(2)}) collective-permute-start(bf16[768,128]{1,0:T(8,128)(2,1)S(1)} %get-tuple-element.34), channel_id=1, source_target_pairs={{0,24},{4,28},{8,16},{12,20},{16,8},{20,12},{24,0},{28,4},{1,25},{... | collective-permute-start | bytes 589832 | tf_op jit(solution)/shard_map/ppermute | solution.py:238
  19.8 6.9 %copy-start.1 = (s32[1024]{0:T(1024)S(1)}, s32[1024]{0:T(1024)}, u32[]{:S(2)}) copy-start(s32[1024]{0:T(1024)} %param.9) | copy-start | bytes 12292

commit v5 on v4

--- a/solution.py
+++ b/solution.py
@@ -87,14 +87,18 @@
     return (total * inverse).astype(BF16)
 
 
-def rest_kernel(inverse, rows, tokens_ref, weight_ref, third_ref, own_ref):
+def rest_kernel(inverse, rows, tokens_ref, weight_ref, third_lo_ref, third_hi_ref, own_ref):
     plane = lax.axis_index("tensor")
-    third_ref[...] = product_rows(tokens_ref, weight_ref, third_block(plane), rows, inverse)
+    third = product_rows(tokens_ref, weight_ref, third_block(plane), rows, inverse)
+    cut = third_lo_ref.shape[0]
+    third_lo_ref[...] = third[:cut]
+    third_hi_ref[...] = third[cut:]
     own_ref[...] = product_rows(tokens_ref, weight_ref, plane, rows, inverse)
 
 
-def relay_kernel(third_ref, near_ref, seed_ref, out_ref):
+def relay_kernel(third_lo_ref, third_hi_ref, near_ref, seed_ref, out_ref):
     outer = is_outer(lax.axis_index("tensor"))
+    cut = third_lo_ref.shape[0]
 
     @pl.when(outer)
     def _():
@@ -102,7 +106,9 @@
 
     @pl.when(jnp.logical_not(outer))
     def _():
-        out_ref[...] = (third_ref[...].astype(F32) + seed_ref[...].astype(F32)).astype(BF16)
+        for span, ref in ((slice(0, cut), third_lo_ref), (slice(cut, None), third_hi_ref)):
+            total = ref[...].astype(F32) + seed_ref[span, :].astype(F32)
+            out_ref[span, :] = total.astype(BF16)
 
 
 def momentum_kernel(step, share, tokens_ref, cot_ref, old_ref, fresh_ref, send_ref, keep_ref):
@@ -170,7 +176,8 @@
     own_ref,
     seed_ref,
     cross_ref,
-    cycle_ref,
+    cycle_lo_ref,
+    cycle_hi_ref,
     last_ref,
     updated_ref,
     keys,
@@ -189,8 +196,10 @@
 
     @pl.when(jnp.logical_not(outer))
     def _():
-        more = cross_ref[...].astype(F32) + cycle_ref[...].astype(F32)
-        keys_ref[...] = (total + more).astype(BF16)
+        cut = cycle_lo_ref.shape[0]
+        for span, ref in ((slice(0, cut), cycle_lo_ref), (slice(cut, None), cycle_hi_ref)):
+            more = cross_ref[span, :].astype(F32) + ref[...].astype(F32)
+            keys_ref[span, :] = (total[span] + more).astype(BF16)
 
     keys_copy = pltpu.make_async_copy(keys_ref, keys, sems.at[1])
     keys_copy.start()
@@ -238,6 +247,8 @@
         return lax.ppermute(value, "dp", [(i, goal(i)) for i in range(n_dp)])
 
     block = shaped(rows, width)
+    cut = rows * 11 // 16
+    halves = [shaped(cut, width), shaped(rows - cut, width)]
     seed, near, tokens, weight, cotangent = call(
         first_kernel,
         (inverse, rows),
@@ -258,8 +269,9 @@
     )
     came = over(send, lambda i: i ^ 1)
 
-    third, own = call(rest_kernel, (inverse, rows), [block] * 2, (tokens, weight))
-    cycle_came = along(third, (2, 0, 3, 1))
+    third_lo, third_hi, own = call(rest_kernel, (inverse, rows), halves + [block], (tokens, weight))
+    lo_came = along(third_lo, (2, 0, 3, 1))
+    hi_came = along(third_hi, (2, 0, 3, 1))
 
     sums = call(pair_kernel, (), [shaped(depth, share)] * n_chips, (keep, came))
     votes = [sums[0]] + [
@@ -267,7 +279,7 @@
         for k in range(1, n_chips)
     ]
 
-    (relay,) = call(relay_kernel, (), [block], (third, near, seed_came))
+    (relay,) = call(relay_kernel, (), [block], (third_lo, third_hi, near, seed_came))
     last_came = along(relay, (1, 3, 0, 2))
 
     input_grad, new_momentum = call(
@@ -288,7 +300,7 @@
         keys_kernel,
         (),
         [block, shaped(depth, share)],
-        (own, seed_came, cross_came, cycle_came, last_came, updated),
+        (own, seed_came, cross_came, lo_came, hi_came, last_came, updated),
         out_specs=[IN_HBM] * 2,
         scratch=[pltpu.VMEM((rows, width), BF16), dma((2,))],
     )
@@ -327,7 +339,8 @@
 
     def per_device(tokens, cotangent, weight, momentum, threshold):
         depth, width = weight.shape
-        fits = n_tensor == 4 and n_dp == 8 and width % (n_dp * LANES) == 0 and depth % TILE == 0
+        fits = n_tensor == 4 and n_dp == 8 and width % (n_dp * LANES) == 0
+        fits = fits and depth % TILE == 0 and tokens.shape[0] % (64 * n_tensor) == 0
         chosen = on_line_of_four if fits else in_general
         return chosen(tokens, cotangent, weight, momentum, threshold)
 

time: 31.4 us -> 32.6 us (1.038)
  starting transfers between devices: 13.4 us -> 14.2 us
  waiting for transfers between devices: 9.71 us -> 10.1 us
    ppermute x4 -> x5, waiting for transfers between devices: 4.6 us -> 10.1 us  [along(): return lax.ppermute(value, ('dp', 'tensor'), pairs)]
    ppermute x4, waiting for transfers between devices: 5.12 us -> 0.01 us  [over(): return lax.ppermute(value, 'dp', [(i, goal(i)) for i in range(n_dp)])]
    ppermute x4, starting transfers between devices: 5.71 us -> 6.7 us  [over(): return lax.ppermute(value, 'dp', [(i, goal(i)) for i in range(n_dp)])]
    ppermute x4 -> x5, starting transfers between devices: 7.68 us -> 7.52 us  [along(): return lax.ppermute(value, ('dp', 'tensor'), pairs)]
  transfers between devices with their start and end apart: 8 -> 9, of which waited for: 3 -> 3; matrix products, arithmetic and copies ran while one was open for 0% -> 0% of each run, Pallas kernels for 9% -> 8%
where the time goes in v5:
time: 32.6 us; the launch traced here: 32.5 us
  starting transfers between devices  14.2 us (44%)
  waiting for transfers between devices  10.1 us (31%)
  Pallas kernels  7.14 us (22%)
  between operations  0.71 us (2%)
    ppermute x5, waiting for transfers between devices, along(): return lax.ppermute(value, ('dp', 'tensor'), pairs)  10.1 us
    ppermute x5, starting transfers between devices, along(): return lax.ppermute(value, ('dp', 'tensor'), pairs)  7.52 us
    pallas_call x8, Pallas kernels, call(): pl.pallas_call(body, out_shape=outs, in_specs=in_specs or [IN_VMEM] * len...  7.14 us
    ppermute x4, starting transfers between devices, over(): return lax.ppermute(value, 'dp', [(i, goal(i)) for i in range(n_dp)])  6.7 us
  transfers between devices with their start and end apart: 9, of which 3 were waited for; matrix products, arithmetic and copies ran while one was open for 0% of the time, Pallas kernels for 8%

profile of v5, /device:TPU:0, one launch (start us, length us, event | category | flops | bytes accessed | tf_op | source)
XLA Modules:
  0.0 32.5 jit_solution(13947971873915469417)
XLA Ops:
  0.6 0.0 copy-start
  0.6 2.2 %shard_map.84 = (bf16[128,1024]{1,0:T(8,128)(2,1)S(1)}, bf16[128,1024]{1,0:T(8,128)(2,1)S(1)}, bf16[512,768]{1,0:T(8,128)(2,1)S(1)}, bf16[768,1024]{1,0:T(8,128)(2,1)S(1)}, bf16[512,1024]{1,0:T(8,128)(2,1)S(1)}) custom-call(bf16[512,768]{1,0:T(8,128)(2,1)} %refs_0_.1, bf16[768,1024]{1,0:T(8,128)(2,1)} %refs_1_.1, bf16[512,1024]{1,0:T(8,128)(2,1)} %refs_2_.2), custom_call_target="tpu_custom_call" | custom-call | tf_op jit(solution)/shard_map/pallas_call | solution.py:218
  2.9 0.3 copy-done
  3.1 1.3 %shard_map.87 = (bf16[768,1024]{1,0:T(8,128)(2,1)S(1)}, bf16[4,768,128]{2,1,0:T(8,128)(2,1)S(1)}, bf16[4,768,128]{2,1,0:T(8,128)(2,1)S(1)}) custom-call(bf16[512,768]{1,0:T(8,128)(2,1)S(1)} %get-tuple-element.23.refs_0_, bf16[512,1024]{1,0:T(8,128)(2,1)S(1)} %get-tuple-element.30.refs_1_.refs_0_, bf16[1,768,1024]{2,1,0:T(8,128)(2,1)S(1)} %copy-done), custom_call_target="tpu_custom_call" | custom-call | tf_op jit(solution)/shard_map/pallas_call | solution.py:218
  4.4 0.6 %collective-permute-start.5 = (bf16[4,768,128]{2,1,0:T(8,128)(2,1)S(1)}, bf16[4,768,128]{2,1,0:T(8,128)(2,1)S(1)}, u32[]{:S(2)}, u32[]{:S(2)}) collective-permute-start(bf16[4,768,128]{2,1,0:T(8,128)(2,1)S(1)} %get-tuple-element.32), channel_id=1, source_target_pairs={{0,4},{4,0},{8,12},{12,8},{16,20},{20,16},{24,28},{28,24},{1,5},{5... | collective-permute-start | bytes 2359304 | tf_op jit(solution)/shard_map/ppermute | solution.py:247
  5.0 2.6 %collective-permute-start = (bf16[128,1024]{1,0:T(8,128)(2,1)S(1)}, bf16[128,1024]{1,0:T(8,128)(2,1)S(1)}, u32[]{:S(2)}, u32[]{:S(2)}) collective-permute-start(bf16[128,1024]{1,0:T(8,128)(2,1)S(1)} %get-tuple-element.26), channel_id=1, source_target_pairs={{0,1},{1,0},{2,3},{3,2},{4,5},{5,4},{6,7},{7,6},{8,9},{9,8},{10,11... | collective-permute-start | bytes 786440 | tf_op jit(solution)/shard_map/ppermute | solution.py:244
  7.6 0.0 collective-permute-done.5.refs_1_
  7.6 0.2 shard_map.88
  7.8 2.2 %collective-permute-start.6 = (bf16[768,128]{1,0:T(8,128)(2,1)S(1)}, bf16[768,128]{1,0:T(8,128)(2,1)S(1)}, u32[]{:S(2)}, u32[]{:S(2)}) collective-permute-start(bf16[768,128]{1,0:T(8,128)(2,1)S(1)} %get-tuple-element.34), channel_id=1, source_target_pairs={{0,8},{4,20},{8,0},{12,28},{16,24},{20,4},{24,16},{28,12},{1,9},{5... | collective-permute-start | bytes 589832 | tf_op jit(solution)/shard_map/ppermute | solution.py:247
  10.0 1.5 %collective-permute-start.7 = (bf16[768,128]{1,0:T(8,128)(2,1)S(1)}, bf16[768,128]{1,0:T(8,128)(2,1)S(1)}, u32[]{:S(2)}, u32[]{:S(2)}) collective-permute-start(bf16[768,128]{1,0:T(8,128)(2,1)S(1)} %get-tuple-element.35), channel_id=1, source_target_pairs={{0,16},{4,12},{8,24},{12,4},{16,0},{20,28},{24,8},{28,20},{1,17},{... | collective-permute-start | bytes 589832 | tf_op jit(solution)/shard_map/ppermute | solution.py:247
  11.5 0.0 collective-permute-start.1
  11.5 0.6 %shard_map.85 = (bf16[88,1024]{1,0:T(8,128)(2,1)S(1)}, bf16[40,1024]{1,0:T(8,128)(2,1)S(1)}, bf16[128,1024]{1,0:T(8,128)(2,1)S(1)}) custom-call(bf16[512,768]{1,0:T(8,128)(2,1)S(1)} %get-tuple-element.23.refs_0_, bf16[768,1024]{1,0:T(8,128)(2,1)S(1)} %get-tuple-element.24.refs_1_.refs_0_), custom_call_target="tpu_custom_call" | custom-call | tf_op jit(solution)/shard_map/pallas_call | solution.py:218
  12.1 2.4 %collective-permute-done.refs_3_.refs_1_ = bf16[128,1024]{1,0:T(8,128)(2,1)S(1)} collective-permute-done((bf16[128,1024]{1,0:T(8,128)(2,1)S(1)}, bf16[128,1024]{1,0:T(8,128)(2,1)S(1)}, u32[]{:S(2)}, u32[]{:S(2)}) %collective-permute-start) | collective-permute-done | bytes 262176 | tf_op jit(solution)/shard_map/ppermute | solution.py:244
  14.6 1.8 %collective-permute-start.4 = (bf16[128,1024]{1,0:T(8,128)(2,1)S(1)}, bf16[128,1024]{1,0:T(8,128)(2,1)S(1)}, u32[]{:S(2)}, u32[]{:S(2)}) collective-permute-start(bf16[128,1024]{1,0:T(8,128)(2,1)S(1)} %shard_map.86), channel_id=1, source_target_pairs={{0,1},{1,3},{2,0},{3,2},{4,5},{5,7},{6,4},{7,6},{8,9},{9,11},{10,8... | collective-permute-start | bytes 786440 | tf_op jit(solution)/shard_map/ppermute | solution.py:244
  16.4 2.4 %collective-permute-start.8 = (bf16[768,128]{1,0:T(8,128)(2,1)S(1)}, bf16[768,128]{1,0:T(8,128)(2,1)S(1)}, u32[]{:S(2)}, u32[]{:S(2)}) collective-permute-start(bf16[768,128]{1,0:T(8,128)(2,1)S(1)} %get-tuple-element.36), channel_id=1, source_target_pairs={{0,24},{4,28},{8,16},{12,20},{16,8},{20,12},{24,0},{28,4},{1,25},{... | collective-permute-start | bytes 589832 | tf_op jit(solution)/shard_map/ppermute | solution.py:247
  18.9 0.0 collective-permute-done.6.refs_3_
  18.9 1.3 %collective-permute-start.2 = (bf16[88,1024]{1,0:T(8,128)(2,1)S(1)}, bf16[88,1024]{1,0:T(8,128)(2,1)S(1)}, u32[]{:S(2)}, u32[]{:S(2)}) collective-permute-start(bf16[88,1024]{1,0:T(8,128)(2,1)S(1)} %get-tuple-element.28.refs_0_), channel_id=1, source_target_pairs={{0,2},{1,0},{2,3},{3,1},{4,6},{5,4},{6,7},{7,5},{8,10},{9,8},{10,1... | collective-permute-start | bytes 540680 | tf_op jit(solution)/shard_map/ppermute | solution.py:244
  20.2 0.0 collective-permute-done.7.refs_4_
  20.2 1.7 %collective-permute-start.3 = (bf16[40,1024]{1,0:T(8,128)(2,1)S(1)}, bf16[40,1024]{1,0:T(8,128)(2,1)S(1)}, u32[]{:S(2)}, u32[]{:S(2)}) collective-permute-start(bf16[40,1024]{1,0:T(8,128)(2,1)S(1)} %get-tuple-element.29.refs_1_), channel_id=1, source_target_pairs={{0,2},{1,0},{2,3},{3,1},{4,6},{5,4},{6,7},{7,5},{8,10},{9,8},{10,1... | collective-permute-start | bytes 245768 | tf_op jit(solution)/shard_map/ppermute | solution.py:244
  21.9 0.0 copy-start.1
  21.9 1.8 %shard_map.91 = (bf16[512,768]{1,0:T(8,128)(2,1)}, bf16[1,768,1024]{2,1,0:T(8,128)(2,1)}) custom-call(bf16[512,1024]{1,0:T(8,128)(2,1)S(1)} %get-tuple-element.30.refs_1_.refs_0_, bf16[768,1024]{1,0:T(8,128)(2,1)S(1)} %get-tuple-element.24.refs_1_.refs_0_, bf16[768,1024]{1,0:T(8,128)(2,1)S(1)} %get-tuple-element.38.refs_2_), custom_call_target="tpu_custom_call" | custom-call | tf_op jit(solution)/shard_map/pallas_call | solution.py:218
  23.7 0.0 collective-permute-done.8.refs_5_
  23.7 0.0 copy-done.1
  23.7 0.2 shard_map.89.refs_6_
  23.9 6.2 %collective-permute-done.3.refs_4_ = bf16[40,1024]{1,0:T(8,128)(2,1)S(1)} collective-permute-done((bf16[40,1024]{1,0:T(8,128)(2,1)S(1)}, bf16[40,1024]{1,0:T(8,128)(2,1)S(1)}, u32[]{:S(2)}, u32[]{:S(2)}) %collective-permute-start.3) | collective-permute-done | bytes 81952 | tf_op jit(solution)/shard_map/ppermute | solution.py:244
  30.1 0.0 collective-permute-done.2.refs_3_
  30.1 0.0 collective-permute-done.1.refs_2_
  30.1 1.5 %collective-permute-done.4.refs_5_ = bf16[128,1024]{1,0:T(8,128)(2,1)S(1)} collective-permute-done((bf16[128,1024]{1,0:T(8,128)(2,1)S(1)}, bf16[128,1024]{1,0:T(8,128)(2,1)S(1)}, u32[]{:S(2)}, u32[]{:S(2)}) %collective-permute-start.4) | collective-permute-done | bytes 262176 | tf_op jit(solution)/shard_map/ppermute | solution.py:244
  31.6 0.9 %shard_map.90 = (bf16[128,1024]{1,0:T(8,128)(2,1)}, bf16[768,128]{1,0:T(8,128)(2,1)}) custom-call(bf16[128,1024]{1,0:T(8,128)(2,1)S(1)} %get-tuple-element.25.refs_0_, bf16[128,1024]{1,0:T(8,128)(2,1)S(1)} %collective-permute-done.refs_3_.refs_1_, bf16[128,1024]{1,0:T(8,128)(2,1)S(1)} %collective-permute-done.1.refs_2_, ...), custom_call_target="tpu_custom_call" | custom-call | tf_op jit(solution)/shard_map/pallas_call | solution.py:218
  (1 shorter events, 0.0 us)
Async XLA Ops:
  0.6 2.5 %copy-start = (bf16[1,768,1024]{2,1,0:T(8,128)(2,1)S(1)}, bf16[1,768,1024]{2,1,0:T(8,128)(2,1)}, u32[]{:S(2)}) copy-start(bf16[1,768,1024]{2,1,0:T(8,128)(2,1)} %refs_2_.3) | copy-start | bytes 4718596
  4.4 3.2 %collective-permute-start.5 = (bf16[4,768,128]{2,1,0:T(8,128)(2,1)S(1)}, bf16[4,768,128]{2,1,0:T(8,128)(2,1)S(1)}, u32[]{:S(2)}, u32[]{:S(2)}) collective-permute-start(bf16[4,768,128]{2,1,0:T(8,128)(2,1)S(1)} %get-tuple-element.32), channel_id=1, source_target_pairs={{0,4},{4,0},{8,12},{12,8},{16,20},{20,16},{24,28},{28,24},{1,5},{5... | collective-permute-start | bytes 2359304 | tf_op jit(solution)/shard_map/ppermute | solution.py:247
  5.0 9.5 %collective-permute-start = (bf16[128,1024]{1,0:T(8,128)(2,1)S(1)}, bf16[128,1024]{1,0:T(8,128)(2,1)S(1)}, u32[]{:S(2)}, u32[]{:S(2)}) collective-permute-start(bf16[128,1024]{1,0:T(8,128)(2,1)S(1)} %get-tuple-element.26), channel_id=1, source_target_pairs={{0,1},{1,0},{2,3},{3,2},{4,5},{5,4},{6,7},{7,6},{8,9},{9,8},{10,11... | collective-permute-start | bytes 786440 | tf_op jit(solution)/shard_map/ppermute | solution.py:244
  7.8 11.0 %collective-permute-start.6 = (bf16[768,128]{1,0:T(8,128)(2,1)S(1)}, bf16[768,128]{1,0:T(8,128)(2,1)S(1)}, u32[]{:S(2)}, u32[]{:S(2)}) collective-permute-start(bf16[768,128]{1,0:T(8,128)(2,1)S(1)} %get-tuple-element.34), channel_id=1, source_target_pairs={{0,8},{4,20},{8,0},{12,28},{16,24},{20,4},{24,16},{28,12},{1,9},{5... | collective-permute-start | bytes 589832 | tf_op jit(solution)/shard_map/ppermute | solution.py:247
  10.0 10.2 %collective-permute-start.7 = (bf16[768,128]{1,0:T(8,128)(2,1)S(1)}, bf16[768,128]{1,0:T(8,128)(2,1)S(1)}, u32[]{:S(2)}, u32[]{:S(2)}) collective-permute-start(bf16[768,128]{1,0:T(8,128)(2,1)S(1)} %get-tuple-element.35), channel_id=1, source_target_pairs={{0,16},{4,12},{8,24},{12,4},{16,0},{20,28},{24,8},{28,20},{1,17},{... | collective-permute-start | bytes 589832 | tf_op jit(solution)/shard_map/ppermute | solution.py:247
  11.5 18.6 %collective-permute-start.1 = (bf16[128,1024]{1,0:T(8,128)(2,1)S(1)}, bf16[128,1024]{1,0:T(8,128)(2,1)S(1)}, u32[]{:S(2)}, u32[]{:S(2)}) collective-permute-start(bf16[128,1024]{1,0:T(8,128)(2,1)S(1)} %get-tuple-element.27.refs_2_), channel_id=1, source_target_pairs={{0,4},{1,2},{2,1},{3,7},{4,0},{5,6},{6,5},{7,3},{8,12},{9,10},{10,... | collective-permute-start | bytes 786440 | tf_op jit(solution)/shard_map/ppermute | solution.py:244
  14.6 17.0 %collective-permute-start.4 = (bf16[128,1024]{1,0:T(8,128)(2,1)S(1)}, bf16[128,1024]{1,0:T(8,128)(2,1)S(1)}, u32[]{:S(2)}, u32[]{:S(2)}) collective-permute-start(bf16[128,1024]{1,0:T(8,128)(2,1)S(1)} %shard_map.86), channel_id=1, source_target_pairs={{0,1},{1,3},{2,0},{3,2},{4,5},{5,7},{6,4},{7,6},{8,9},{9,11},{10,8... | collective-permute-start | bytes 786440 | tf_op jit(solution)/shard_map/ppermute | solution.py:244
  16.4 7.3 %collective-permute-start.8 = (bf16[768,128]{1,0:T(8,128)(2,1)S(1)}, bf16[768,128]{1,0:T(8,128)(2,1)S(1)}, u32[]{:S(2)}, u32[]{:S(2)}) collective-permute-start(bf16[768,128]{1,0:T(8,128)(2,1)S(1)} %get-tuple-element.36), channel_id=1, source_target_pairs={{0,24},{4,28},{8,16},{12,20},{16,8},{20,12},{24,0},{28,4},{1,25},{... | collective-permute-start | bytes 589832 | tf_op jit(solution)/shard_map/ppermute | solution.py:247
  18.9 11.2 %collective-permute-start.2 = (bf16[88,1024]{1,0:T(8,128)(2,1)S(1)}, bf16[88,1024]{1,0:T(8,128)(2,1)S(1)}, u32[]{:S(2)}, u32[]{:S(2)}) collective-permute-start(bf16[88,1024]{1,0:T(8,128)(2,1)S(1)} %get-tuple-element.28.refs_0_), channel_id=1, source_target_pairs={{0,2},{1,0},{2,3},{3,1},{4,6},{5,4},{6,7},{7,5},{8,10},{9,8},{10,1... | collective-permute-start | bytes 540680 | tf_op jit(solution)/shard_map/ppermute | solution.py:244
  20.2 9.9 %collective-permute-start.3 = (bf16[40,1024]{1,0:T(8,128)(2,1)S(1)}, bf16[40,1024]{1,0:T(8,128)(2,1)S(1)}, u32[]{:S(2)}, u32[]{:S(2)}) collective-permute-start(bf16[40,1024]{1,0:T(8,128)(2,1)S(1)} %get-tuple-element.29.refs_1_), channel_id=1, source_target_pairs={{0,2},{1,0},{2,3},{3,1},{4,6},{5,4},{6,7},{7,5},{8,10},{9,8},{10,1... | collective-permute-start | bytes 245768 | tf_op jit(solution)/shard_map/ppermute | solution.py:244
  21.9 1.8 %copy-start.1 = (s32[1024]{0:T(1024)S(1)}, s32[1024]{0:T(1024)}, u32[]{:S(2)}) copy-start(s32[1024]{0:T(1024)} %param.9) | copy-start | bytes 12292
